TPU v7x, 512 devices: a whole 4x4x16 slice. The times are simulated.
512 devices in a mesh: width: 16 (over z), cb: 16 (over x, y), row: 2 (over core).
Axes of the slice: x: 4, y: 4, z: 16, core: 2. Of those that a mesh axis runs over, the one named last changes fastest.
Arguments:
- weights: bfloat16 [14336, 8192], P(('cb', 'row'), 'width'), as said below
- dir_codes: int32 [14336, 1024], P(('cb', 'row'), 'width'), may hold values from 0 to 65535
- norm_bins: int32 [14336, 1024], P(('cb', 'row'), 'width'), may hold values from 0 to 255, as said below
Outputs:
- codewords: float32 [4096, 128], P('cb')
- norm_levels: float32 [256], replicated
Inputs may be any that keep to these rules, and one draw needn't show every extreme that they name: `weights`: real-valued entries, rows of differing scales. `norm_bins`: the bins of one row all lie in one aligned run of 16 consecutive bins.
All inputs are finite; a program needn't handle non-finite values.
Results may differ from a plain program's by a relative error of at most 0.0003.
Values sent between devices are 32-bit elements; how exact they have to be, the bound alone decides.
No kernel may reach another device: no remote copies, remote signals or barrier semaphores. Data moves between devices by JAX's collectives and lax.ppermute only.
A program may use at most 128 MiB of HBM per device.

v0:
```python
import math

import jax
import jax.numpy as jnp
from jax import lax
from jax.sharding import PartitionSpec as P

WIDTH = 8192
CODES = 65536
NBINS = 256


def swapped(array, axis, distance):
    return lax.ppermute(array, axis, [(i, i ^ 1 << distance) for i in range(lax.axis_size(axis))])


def sylvester(matrix_order, out_type):
    indices = jnp.arange(matrix_order, dtype=jnp.int32)
    common = jnp.bitwise_and(indices[:, None], indices[None, :])
    bit_total = jnp.zeros((matrix_order, matrix_order), jnp.int32)
    for bit_place in range(max(matrix_order.bit_length() - 1, 0)):
        bit_total = bit_total + jnp.bitwise_and(jnp.right_shift(common, bit_place), 1)
    parity = bit_total % 2
    return (1 - 2 * parity).astype(out_type)


def bin_totals(log_norms, bin_ids):
    group_count = log_norms.shape[0]
    block_count = 8
    block_size = group_count // block_count
    bin_range = jnp.arange(NBINS, dtype=jnp.int32)

    def accumulate(running, block_item):
        block_logs, block_bins = block_item
        onehot = (block_bins[:, None] == bin_range[None, :]).astype(jnp.float32)
        values = jnp.stack([block_logs, jnp.ones_like(block_logs)], axis=0)
        block_part = jnp.dot(values, onehot, precision=lax.Precision.HIGHEST)
        return (running + block_part, None)

    block_items = (
        log_norms.reshape(block_count, block_size),
        bin_ids.reshape(block_count, block_size),
    )
    running, _ = lax.scan(accumulate, jnp.zeros((2, NBINS), jnp.float32), block_items)
    return (running[0], running[1])


def per_device(weights, dir_codes, norm_bins):
    row_count, col_count = weights.shape
    scaling = 1.0 / math.sqrt(WIDTH)
    width_devices = lax.axis_size("width")
    local_part = jnp.dot(
        weights, sylvester(col_count, jnp.bfloat16), preferred_element_type=jnp.float32
    )
    position = lax.axis_index("width")
    for level_bit in range(width_devices.bit_length() - 1):
        partner = swapped(local_part, "width", level_bit)
        upper_half = position // 2**level_bit % 2 == 1
        local_part = jnp.where(upper_half, partner - local_part, local_part + partner)
    rotated = local_part * scaling
    grouped = rotated.reshape(-1, 8)
    code_flat = dir_codes.reshape(-1)
    bin_flat = norm_bins.reshape(-1)
    group_norms = jnp.sqrt(jnp.sum(grouped * grouped, axis=-1))
    floored = jnp.maximum(group_norms, 1.0)
    directions = grouped / floored[:, None]
    log_norms = jnp.log(floored)
    bin_sums, bin_counts = bin_totals(log_norms, bin_flat)
    total_sums, total_counts = lax.psum((bin_sums, bin_counts), ("width", "cb", "row"))
    norm_levels = total_sums / jnp.maximum(total_counts, 1.0)
    partial_value = jax.ops.segment_sum(directions, code_flat, num_segments=CODES).reshape(-1)
    owned_sums = lax.psum_scatter(partial_value, "cb", scatter_dimension=0, tiled=True)
    code_totals = lax.psum(owned_sums, ("width", "row"))
    summed = code_totals.reshape(-1, 8)
    lengths = jnp.sqrt(jnp.sum(summed * summed, axis=-1))
    codewords = (summed / jnp.maximum(lengths, 1.0)[:, None]).reshape(-1, 128)
    return (codewords, norm_levels)


def solution(mesh):
    return jax.shard_map(
        per_device,
        mesh=mesh,
        in_specs=(P(("cb", "row"), "width"), P(("cb", "row"), "width"), P(("cb", "row"), "width")),
        out_specs=(P("cb", None), P()),
        check_vma=False,
    )
```

profile of v0, /device:TPU:1, one launch (start us, length us, event | category | flops | bytes accessed | tf_op | source)
XLA Modules:
  0.0 833.0 jit_solution(2835986889016512261)
XLA Ops:
  7.2 0.0 copy-start
  7.2 0.0 copy-start.1
  7.2 0.0 copy-start.2
  7.2 0.0 all-reduce.8.cloned.1.call-start
  7.2 0.9 copy-done
  8.2 2.2 convolution_bitcast_fusion
  10.4 4.4 collective-permute-start
  14.8 15.6 %collective-permute-done = f32[448,512]{1,0:T(8,128)S(1)} collective-permute-done((f32[448,512]{1,0:T(8,128)S(1)}, f32[448,512]{1,0:T(8,128)S(1)}, u32[]{:S(2)}, u32[]{:S(2)}) %collective-permute-start) | collective-permute-done | bytes 917536 | tf_op jit(solution)/shard_map/ppermute | solution.py:14
  30.4 0.2 add_select_fusion.3
  30.6 9.3 %collective-permute-start.1 = (f32[448,512]{1,0:T(8,128)S(1)}, f32[448,512]{1,0:T(8,128)S(1)}, u32[]{:S(2)}, u32[]{:S(2)}) collective-permute-start(f32[448,512]{1,0:T(8,128)S(1)} %add_select_fusion.3), channel_id=1, source_target_pairs={{0,64},{32,96},{64,0},{96,32},{128,192},{160,224},{192,128},{224,1... | collective-permute-start | bytes 2752520 | tf_op jit(solution)/shard_map/ppermute | solution.py:14
  39.9 39.4 %collective-permute-done.1 = f32[448,512]{1,0:T(8,128)S(1)} collective-permute-done((f32[448,512]{1,0:T(8,128)S(1)}, f32[448,512]{1,0:T(8,128)S(1)}, u32[]{:S(2)}, u32[]{:S(2)}) %collective-permute-start.1) | collective-permute-done | bytes 917536 | tf_op jit(solution)/shard_map/ppermute | solution.py:14
  79.3 0.2 add_select_fusion.2
  79.5 8.8 %collective-permute-start.2 = (f32[448,512]{1,0:T(8,128)S(1)}, f32[448,512]{1,0:T(8,128)S(1)}, u32[]{:S(2)}, u32[]{:S(2)}) collective-permute-start(f32[448,512]{1,0:T(8,128)S(1)} %add_select_fusion.2), channel_id=1, source_target_pairs={{0,128},{32,160},{64,192},{96,224},{128,0},{160,32},{192,64},{224,... | collective-permute-start | bytes 2752520 | tf_op jit(solution)/shard_map/ppermute | solution.py:14
  88.4 98.6 %collective-permute-done.2 = f32[448,512]{1,0:T(8,128)S(1)} collective-permute-done((f32[448,512]{1,0:T(8,128)S(1)}, f32[448,512]{1,0:T(8,128)S(1)}, u32[]{:S(2)}, u32[]{:S(2)}) %collective-permute-start.2) | collective-permute-done | bytes 917536 | tf_op jit(solution)/shard_map/ppermute | solution.py:14
  187.0 0.2 add_select_fusion.1
  187.2 52.4 %collective-permute-start.3 = (f32[448,512]{1,0:T(8,128)S(1)}, f32[448,512]{1,0:T(8,128)S(1)}, u32[]{:S(2)}, u32[]{:S(2)}) collective-permute-start(f32[448,512]{1,0:T(8,128)S(1)} %add_select_fusion.1), channel_id=1, source_target_pairs={{0,256},{32,288},{64,320},{96,352},{128,384},{160,416},{192,448},{... | collective-permute-start | bytes 2752520 | tf_op jit(solution)/shard_map/ppermute | solution.py:14
  239.6 0.0 copy-done.1
  239.6 0.1 copy.17
  239.7 0.1 reshape_reshape.3
  239.9 0.0 copy-done.2
  239.9 0.1 copy.14
  240.0 0.1 reshape.45
  240.1 1.3 dynamic-slice
  242.0 37.4 %collective-permute-done.3 = f32[448,512]{1,0:T(8,128)S(1)} collective-permute-done((f32[448,512]{1,0:T(8,128)S(1)}, f32[448,512]{1,0:T(8,128)S(1)}, u32[]{:S(2)}, u32[]{:S(2)}) %collective-permute-start.3) | collective-permute-done | bytes 917536 | tf_op jit(solution)/shard_map/ppermute | solution.py:14
  279.4 0.2 select_multiply_fusion
  279.6 9.9 %reshape.40 = f32[28672,8]{1,0:T(8,128)} reshape(f32[448,512]{1,0:T(8,128)S(1)} %select_multiply_fusion) | data formatting | bytes 1835008 | tf_op jit(solution)/shard_map/reshape | solution.py:61
  289.5 7.5 multiply_reduce_fusion
  297.0 0.1 fusion.34
  297.1 180.9 %scatter_custom_fusion = f32[65536,8]{1,0:T(8,128)} fusion(s32[28672]{0:T(1024)S(1)} %reshape.45, f32[]{:T(128)} %constant.99.clone.1, f32[28672,8]{1,0:T(8,128)} %reshape.40, f32[28672]{0:T(1024)S(1)} %get-tuple-element.60), kind=kCustom, calls=%fused_computation.10 | custom fusion | flops 458752 | bytes 3129348 | tf_op jit(solution)/shard_map/scatter-add | solution.py:71
  478.0 23.7 %reshape.41 = f32[524288]{0:T(1024)} reshape(f32[65536,8]{1,0:T(8,128)} %scatter_custom_fusion) | data formatting | bytes 4194304 | tf_op jit(solution)/shard_map/reshape | solution.py:71
  501.7 0.0 all-reduce.8.cloned.1.call-update
  501.7 0.0 all-reduce.6.cloned.1.call-start
  501.8 10.8 %while.11 = (s32[]{:T(128)}, f32[2,256]{1,0:T(2,128)S(1)}, f32[8,3584]{1,0:T(8,128)S(1)}, s32[8,3584]{1,0:T(8,128)S(1)}, s32[]{:T(128)}, /*index=5*/s32[]{:T(128)}) while((s32[]{:T(128)}, f32[2,256]{1,0:T(2,128)S(1)}, f32[8,3584]{1,0:T(8,128)S(1)}, s32[8,3584]{1,0:T(8,128)S(1)}, s32[]{:T(128)}, /*index=5*/s32[]{:T(128)}) %tuple.29), condition=%wide.region_6.7_spmd.clone, body=%wide.region_5.6_spmd.clone.sunk | while | flops 22938628 | bytes 90199 | solution.py:44
  501.9 1.3 fusion.40
  503.2 1.3 fusion.40
  504.6 1.3 fusion.40
  505.9 1.3 fusion.40
  507.3 1.3 fusion.40
  508.6 1.3 fusion.40
  510.0 1.3 fusion.40
  511.3 1.3 fusion.40
  512.6 101.9 %all-reduce.2 = (f32[256]{0:T(256)S(1)}, f32[256]{0:T(256)S(1)}) all-reduce(f32[256]{0:T(256)S(1)} %bitcast.11, f32[256]{0:T(256)S(1)} %bitcast.10), channel_id=1, replica_groups=mesh['width'=16,'cb'=16,'row'=2] {'width','cb','row'}, use_global_device_ids=true, to_apply=%region_7.8 | all-reduce | flops 512 | bytes 4096 | tf_op jit(solution)/shard_map/psum | solution.py:69
  614.5 3.5 all-reduce.8.cloned.1.call-done
  618.0 1.6 dynamic-slice.1
  619.6 0.0 all-reduce.6.cloned.1.call-update
  619.6 0.6 maximum_divide_fusion
  620.2 201.4 %all-reduce.6.cloned.1.call-done = f32[32768]{0:T(1024)} async-done(((f32[32768]{0:T(1024)}), f32[32768]{0:T(1024)}) %all-reduce.6.cloned.1.call-update) | async-done | bytes 131088 | tf_op jit(solution)/shard_map/psum | solution.py:73
  821.5 1.0 mul.22
  822.5 1.1 mul.23
  823.7 0.6 reduce_sum.19
  824.3 0.1 max.35
  824.4 0.1 copy.15
  824.5 0.1 copy.16
  824.6 1.6 bitcast_divide_fusion
  (21 shorter events, 0.6 us)
Async XLA Ops:
  7.2 1.0 copy-start
  7.2 232.4 %copy-start.1 = (s32[448,64]{0,1:T(8,128)S(1)}, s32[448,64]{0,1:T(8,128)}, u32[]{:S(2)}) copy-start(s32[448,64]{0,1:T(8,128)} %param.7) | copy-start | bytes 344068
  7.2 232.7 %copy-start.2 = (s32[448,64]{0,1:T(8,128)S(1)}, s32[448,64]{0,1:T(8,128)}, u32[]{:S(2)}) copy-start(s32[448,64]{0,1:T(8,128)} %param.6) | copy-start | bytes 344068
  7.2 610.8 %all-reduce.8.cloned.1.call-start = ((), (), s32[]{:S(2)}) async-start(), calls=%async_computation.1 | async-start | bytes 4194304
  10.4 19.9 %collective-permute-start = (f32[448,512]{1,0:T(8,128)S(1)}, f32[448,512]{1,0:T(8,128)S(1)}, u32[]{:S(2)}, u32[]{:S(2)}) collective-permute-start(f32[448,512]{1,0:T(8,128)S(1)} %convolution_bitcast_fusion), channel_id=1, source_target_pairs={{0,32},{32,0},{64,96},{96,64},{128,160},{160,128},{192,224},{224,1... | collective-permute-start | bytes 2752520 | tf_op jit(solution)/shard_map/ppermute | solution.py:14
  30.6 48.7 %collective-permute-start.1 = (f32[448,512]{1,0:T(8,128)S(1)}, f32[448,512]{1,0:T(8,128)S(1)}, u32[]{:S(2)}, u32[]{:S(2)}) collective-permute-start(f32[448,512]{1,0:T(8,128)S(1)} %add_select_fusion.3), channel_id=1, source_target_pairs={{0,64},{32,96},{64,0},{96,32},{128,192},{160,224},{192,128},{224,1... | collective-permute-start | bytes 2752520 | tf_op jit(solution)/shard_map/ppermute | solution.py:14
  79.5 107.4 %collective-permute-start.2 = (f32[448,512]{1,0:T(8,128)S(1)}, f32[448,512]{1,0:T(8,128)S(1)}, u32[]{:S(2)}, u32[]{:S(2)}) collective-permute-start(f32[448,512]{1,0:T(8,128)S(1)} %add_select_fusion.2), channel_id=1, source_target_pairs={{0,128},{32,160},{64,192},{96,224},{128,0},{160,32},{192,64},{224,... | collective-permute-start | bytes 2752520 | tf_op jit(solution)/shard_map/ppermute | solution.py:14
  187.2 92.2 %collective-permute-start.3 = (f32[448,512]{1,0:T(8,128)S(1)}, f32[448,512]{1,0:T(8,128)S(1)}, u32[]{:S(2)}, u32[]{:S(2)}) collective-permute-start(f32[448,512]{1,0:T(8,128)S(1)} %add_select_fusion.1), channel_id=1, source_target_pairs={{0,256},{32,288},{64,320},{96,352},{128,384},{160,416},{192,448},{... | collective-permute-start | bytes 2752520 | tf_op jit(solution)/shard_map/ppermute | solution.py:14
  501.7 319.8 %all-reduce.6.cloned.1.call-start = ((), (), s32[]{:S(2)}) async-start(), calls=%async_computation | async-start | bytes 262144 | tf_op jit(solution)/shard_map/psum | solution.py:73
Sparse Core Ops, SparseCore 0:
  501.8 116.1 all-reduce.7
  620.9 200.6 all-reduce.5
where the time goes:
time: 834 us; the launch traced here: 833 us
  waiting for transfers between devices  396 us (47%)
  other arithmetic  193 us (23%)
  blocking collectives  102 us (12%)
  starting transfers between devices  74.9 us (9%)
  local copies, waits for them, and re-layouts  39.8 us (5%)
  between operations  15 us (2%)
  matrix products  12.4 us (1%)
    psum x1, waiting for transfers between devices, per_device(): code_totals = lax.psum(owned_sums, ('width', 'row'))  201 us
    ppermute x4, waiting for transfers between devices, swapped(): lax.ppermute(array, axis, [(i, i ^ 1 << distance) for i in range(lax.axis...  191 us
    scatter-add x1, other arithmetic, per_device(): jax.ops.segment_sum(directions, code_flat, num_segments=CODES).reshape(-1)  181 us
    psum x1, blocking collectives, per_device(): lax.psum((bin_sums, bin_counts), ('width', 'cb', 'row'))  102 us
    ppermute x4, starting transfers between devices, swapped(): lax.ppermute(array, axis, [(i, i ^ 1 << distance) for i in range(lax.axis...  74.8 us
    reshape x1, local copies, waits for them, and re-layouts, per_device(): jax.ops.segment_sum(directions, code_flat, num_segments=CODES).reshape(-1)  23.7 us
  transfers between devices with their start and end apart: 6, of which 6 were waited for; matrix products, arithmetic and copies ran while one was open for 2% of the time, Pallas kernels for 0%

commit v1 on v0

v1 whole, which is shorter than its diff:
```python
import math

import jax
import jax.numpy as jnp
from jax import lax
from jax.experimental import pallas as pl
from jax.experimental.pallas import tpu as pltpu
from jax.sharding import PartitionSpec as P

WIDTH = 8192
CODES = 65536
NBINS = 256
SCALING = 1.0 / math.sqrt(WIDTH)
F32 = jnp.float32
I32 = jnp.int32

SOURCES = 16
TILES = 14
CHUNKS = 1
ACCS = 8
CODE_ROWS = CODES // 16


def iota(shape, axis):
    return lax.broadcasted_iota(I32, shape, axis)


def lanes_at(values, index):
    return jnp.take_along_axis(values, index, axis=1, mode="promise_in_bounds")


def vmem(count):
    return [pl.BlockSpec(memory_space=pltpu.VMEM)] * count


def pack_kernel(weights_ref, codes_ref, bins_ref, parts_ref, ints_ref):
    common = jnp.bitwise_and(iota((128, 128), 0), iota((128, 128), 1))
    for shift in (4, 2, 1):
        common = jnp.bitwise_xor(common, common >> shift)
    hadamard = (1 - 2 * jnp.bitwise_and(common, 1)).astype(F32).astype(jnp.bfloat16)
    blocks = [
        jnp.dot(weights_ref[:, 128 * b : 128 * b + 128], hadamard, preferred_element_type=F32)
        for b in range(4)
    ]
    sums = [blocks[0] + blocks[1], blocks[0] - blocks[1], blocks[2] + blocks[3], blocks[2] - blocks[3]]
    blocks = [sums[0] + sums[2], sums[1] + sums[3], sums[0] - sums[2], sums[1] - sums[3]]
    for b in range(4):
        parts_ref[:, b] = blocks[b].reshape(56, 8, 128)
    lane = iota((8, 128), 1)
    own = jnp.bitwise_and(lane, 7) == iota((8, 128), 0)

    def spread(ref, tile):
        padded = jnp.concatenate([ref[pl.ds(pl.multiple_of(tile * 8, 8), 8), :]] * 2, axis=1)
        rows = []
        for b in range(4):
            taken = lanes_at(padded, 16 * b + (lane >> 3))
            rows.append(jnp.sum(jnp.where(own, taken, 0), axis=0, keepdims=True))
        return rows

    def step(tile, carry):
        ints_ref[tile] = jnp.concatenate(spread(codes_ref, tile) + spread(bins_ref, tile), axis=0)
        return carry

    lax.fori_loop(0, 56, step, 0)


def pack(weights, codes, bins):
    return pl.pallas_call(
        pack_kernel,
        out_shape=[
            jax.ShapeDtypeStruct((56, 4, 8, 128), F32),
            jax.ShapeDtypeStruct((56, 8, 128), I32),
        ],
        in_specs=vmem(3),
        out_specs=vmem(2),
        name="pack",
    )(weights, codes, bins)


def sums_kernel(tiles, first, *refs):
    side_ref, at_ref, parts_ref, codes_ref, bins_ref = refs[:5]
    before = refs[5:8] if not first else None
    keep_ref, send_ref, totals_ref = refs[-4 - 2 * 1 - ACCS : -3 - ACCS]
    items, directions_ref = refs[-3 - ACCS : -1 - ACCS], refs[-1 - ACCS]
    accs = refs[-ACCS:]
    lane = iota((8, 128), 1)
    place = iota((8, 128), 0)
    inner = jnp.bitwise_and(lane, 7)
    outer = lane >> 3
    for acc in accs:
        acc[...] = jnp.zeros_like(acc)
    group = (iota((128, 128), 0) >> 3 == iota((128, 128), 1) >> 3).astype(F32)

    def rotate(t, carry):
        z = [parts_ref[h, t] for h in range(SOURCES)]
        for bit in range(4):
            d = 1 << bit
            z = [z[h ^ d] - z[h] if h & d else z[h] + z[h ^ d] for h in range(SOURCES)]
        rotated = jnp.concatenate(z, axis=0) * SCALING
        squares = jnp.dot(
            rotated * rotated, group, precision=lax.Precision.HIGHEST, preferred_element_type=F32
        )
        floored = jnp.maximum(jnp.sqrt(squares), 1.0)
        directions = rotated / floored
        logs = jnp.log(floored)
        packed = []
        for half in range(2):
            log_sum = jnp.zeros((8, 128), F32)
            bin_sum = jnp.zeros((8, 128), I32)
            for j in range(8):
                h = 8 * half + j
                bins = jnp.broadcast_to(bins_ref[h, pl.ds(t, 1), :], (8, 128))
                bins = lanes_at(bins, 8 * outer + place)
                log_sum = log_sum + jnp.where(inner == j, logs[8 * h : 8 * h + 8], 0.0)
                bin_sum = bin_sum + jnp.where(inner == j, bins, 0)
            packed.append((log_sum, bin_sum))
        for h in range(SOURCES):
            directions_ref[h * tiles + t] = directions[8 * h : 8 * h + 8]
        base = packed[0][1] >> 4
        low, high, low_count, high_count = carry
        for offset in range(16):
            log_total = jnp.zeros((8, 128), F32)
            count = jnp.zeros((8, 128), F32)
            for log_sum, bin_sum in packed:
                chosen = jnp.bitwise_and(bin_sum, 15) == offset
                log_total = log_total + jnp.where(chosen, log_sum, 0.0)
                count = count + jnp.where(chosen, 1.0, 0.0)
            log_total = jnp.sum(log_total, axis=1, keepdims=True)
            count = jnp.sum(count, axis=1, keepdims=True)
            target = 16 * base + offset
            at_low, at_high = target == lane, target == lane + 128
            low = low + jnp.where(at_low, log_total, 0.0)
            high = high + jnp.where(at_high, log_total, 0.0)
            low_count = low_count + jnp.where(at_low, count, 0.0)
            high_count = high_count + jnp.where(at_high, count, 0.0)
        return low, high, low_count, high_count

    empty = jnp.zeros((8, 128), F32)
    bin_parts = lax.fori_loop(0, tiles, rotate, (empty,) * 4)
    rows = [jnp.sum(part, axis=0, keepdims=True) for part in bin_parts]
    totals = jnp.concatenate(rows + [jnp.zeros((4, 128), F32)], axis=0)

    def lay_out(n, items_ref):
        h, t = n // tiles, n % tiles
        direction = directions_ref[n]
        codes = jnp.broadcast_to(codes_ref[h, pl.ds(t, 1), :], (8, 128))
        codes = jnp.bitwise_and(codes, 15)
        for k in range(16):
            values = lanes_at(direction, 8 * k + inner)
            slot = lanes_at(codes, 8 * k + place)
            items_ref[8 * k : 8 * k + 8, :] = jnp.where(slot == outer, values, 0.0)

    def add(n, items_ref):
        for k in range(16):
            at = [at_ref[n * 128 + 8 * k + s] for s in range(ACCS)]
            old = [accs[s][pl.ds(at[s], 1), :] for s in range(ACCS)]
            for s in range(ACCS):
                accs[s][pl.ds(at[s], 1), :] = old[s] + items_ref[8 * k + s : 8 * k + s + 1, :]

    count = SOURCES * tiles
    lay_out(0, items[0])

    def step(i, carry):
        n = 2 * i
        lay_out(n + 1, items[1])
        add(n, items[0])
        lay_out(jnp.minimum(n + 2, count - 1), items[0])
        add(n + 1, items[1])
        return carry

    lax.fori_loop(0, count // 2, step, 0)
    side = side_ref[0]

    def finish(c, carry):
        for ref, mine in ((keep_ref, side), (send_ref, 1 - side)):
            start = pl.multiple_of(c * 256 + mine * 128, 128)
            total = accs[0][pl.ds(start, 128), :]
            for acc in accs[1:]:
                total = total + acc[pl.ds(start, 128), :]
            if before is not None:
                total = total + before[0 if ref is keep_ref else 1][c]
            ref[c] = total
        return carry

    lax.fori_loop(0, CODE_ROWS // 256, finish, 0)
    totals_ref[...] = totals if before is None else totals + before[2][...]


def direction_sums(side, at, parts, codes, bins, before):
    owners = CODE_ROWS // 256
    tiles = parts.shape[1]
    arrays = () if before is None else tuple(before)

    def kernel(*refs):
        inputs, rest = refs[: 5 + len(arrays)], refs[5 + len(arrays) :]
        sums_kernel(tiles, before is None, *inputs, *rest)

    return pl.pallas_call(
        kernel,
        out_shape=[
            jax.ShapeDtypeStruct((owners, 128, 128), F32),
            jax.ShapeDtypeStruct((owners, 128, 128), F32),
            jax.ShapeDtypeStruct((8, 128), F32),
        ],
        in_specs=[pl.BlockSpec(memory_space=pltpu.SMEM)] * 2 + vmem(3 + len(arrays)),
        out_specs=vmem(3),
        scratch_shapes=[pltpu.VMEM((128, 128), F32)] * 2
        + [pltpu.VMEM((SOURCES * tiles, 8, 128), F32)]
        + [pltpu.VMEM((CODE_ROWS, 128), F32)] * ACCS,
        cost_estimate=pl.CostEstimate(flops=10**9, bytes_accessed=40 * 10**6, transcendentals=0),
        name="sums",
    )(side, at, parts, codes, bins, *arrays)


def join_kernel(keep_ref, got_ref, totals_ref, other_ref, out_ref):
    out_ref[:, :128] = keep_ref[...] + got_ref[...]
    totals = totals_ref[...] + other_ref[...]
    out_ref[:, 128:] = jnp.broadcast_to(totals[None], (out_ref.shape[0], 8, 128))


def owned_kernel(parts_ref, out_ref):
    total = parts_ref[0]
    for c in range(1, parts_ref.shape[0]):
        total = total + parts_ref[c]
    for z in range(SOURCES):
        out_ref[z, :8] = total[8 * z : 8 * z + 8]
        out_ref[z, 8:] = total[128:]


def finish_kernel(parts_ref, words_ref, levels_ref):
    total = parts_ref[0]
    for z in range(1, SOURCES):
        total = total + parts_ref[z]
    summed = total[:8]
    group = (iota((128, 128), 0) >> 3 == iota((128, 128), 1) >> 3).astype(F32)
    squares = jnp.dot(
        summed * summed, group, precision=lax.Precision.HIGHEST, preferred_element_type=F32
    )
    words = summed / jnp.maximum(jnp.sqrt(squares), 1.0)
    for z in range(SOURCES):
        words_ref[z] = words
    levels_ref[...] = total[8:10] / jnp.maximum(total[10:12], 1.0)


def simple(kernel, name, shapes, *arrays):
    out_shape = [jax.ShapeDtypeStruct(shape, F32) for shape in shapes]
    return pl.pallas_call(
        kernel, out_shape=out_shape, in_specs=vmem(len(arrays)), out_specs=vmem(len(shapes)), name=name
    )(*arrays)


def exchanged(array, axis):
    return lax.all_to_all(array, axis, 0, 0, tiled=True)


def per_device(weights, dir_codes, norm_bins):
    owners = CODE_ROWS // 256
    side = lax.axis_index("row")
    parts, ints = pack(weights, dir_codes, norm_bins)
    parts = parts.reshape(SOURCES, TILES, 8, 128)
    ints = ints.reshape(56, 2, 4, 128).transpose(1, 0, 2, 3).reshape(2, SOURCES, TILES, 128)
    tiles = TILES // CHUNKS
    sums = None
    received = []
    for chunk in range(CHUNKS):
        span = slice(chunk * tiles, (chunk + 1) * tiles)
        gap = jnp.zeros((SOURCES, 16 - tiles, 128), I32)
        lists = jnp.concatenate([ints[0, :, span], gap, ints[1, :, span], gap], axis=1)
        received.append((exchanged(lists, "width"), exchanged(parts[:, span], "width")))
    for lists, chunk_parts in received:
        codes, bins = lists[:, :tiles], lists[:, 16 : 16 + tiles]
        at = (codes >> 4).reshape(-1)
        sums = direction_sums(side.reshape(1), at, chunk_parts, codes, bins, sums)
    keep, send, totals = sums
    swap = [(0, 1), (1, 0)]
    got = lax.ppermute(send, "row", swap)
    other = lax.ppermute(totals, "row", swap)
    (joined,) = simple(join_kernel, "join", [(owners, 136, 128)], keep, got, totals, other)
    joined = exchanged(joined, "cb")
    (owned,) = simple(owned_kernel, "owned", [(SOURCES, 16, 128)], joined)
    owned = exchanged(owned, "width")
    words, levels = simple(finish_kernel, "finish", [(SOURCES, 8, 128), (2, 128)], owned)
    mine = exchanged(words, "width").reshape(128, 128)
    theirs = lax.ppermute(mine, "row", swap)
    first = side == 0
    codewords = jnp.concatenate(
        [jnp.where(first, mine, theirs), jnp.where(first, theirs, mine)], axis=0
    )
    return codewords, levels.reshape(NBINS)


def solution(mesh):
    return jax.shard_map(
        per_device,
        mesh=mesh,
        in_specs=(P(("cb", "row"), "width"),) * 3,
        out_specs=(P("cb", None), P()),
        check_vma=False,
    )
```

time: 834 us -> 228 us (0.27)
  waiting for transfers between devices: 396 us -> 40.5 us
  other arithmetic: 193 us -> 1.44 us
  Pallas kernels: 0 us -> 62.8 us
  starting transfers between devices: 74.9 us -> 24.6 us
  local copies, waits for them, and re-layouts: 39.8 us -> 7.12 us
  between operations: 15 us -> 0.73 us
  matrix products: 12.4 us -> 0 us
  blocking collectives: 102 us -> 90.6 us
    psum x1 -> x0, waiting for transfers between devices: 201 us -> none  [per_device(): code_totals = lax.psum(owned_sums, ('width', 'row'))]
    ppermute x4 -> x3, waiting for transfers between devices: 191 us -> 2.22 us  [the longest x1 1.34 us: per_device(): other = lax.ppermute(totals, 'row', swap)]
    scatter-add x1 -> x0, other arithmetic: 181 us -> none  [per_device(): jax.ops.segment_sum(directions, code_flat, num_segments=CODES).reshape(-1)]
    psum x1 -> x0, blocking collectives: 102 us -> none  [per_device(): lax.psum((bin_sums, bin_counts), ('width', 'cb', 'row'))]
    all_to_all x0 -> x4, blocking collectives: none -> 90.6 us  [exchanged(): return lax.all_to_all(array, axis, 0, 0, tiled=True)]
    pallas_call x0 -> x5, Pallas kernels: none -> 62.8 us  [the longest x1 44.8 us: direction_sums(): pl.pallas_call(kernel, out_shape=[jax.ShapeDtypeStruct((owners, 128, 128)...]
    ppermute x4 -> x3, starting transfers between devices: 74.8 us -> 14.2 us  [the longest x1 7.08 us: per_device(): got = lax.ppermute(send, 'row', swap)]
    all_to_all x0 -> x1, waiting for transfers between devices: none -> 38.3 us  [exchanged(): return lax.all_to_all(array, axis, 0, 0, tiled=True)]
  transfers between devices with their start and end apart: 6 -> 4, of which waited for: 6 -> 3; matrix products, arithmetic and copies ran while one was open for 2% -> 1% of each run, Pallas kernels for 0% -> 0%
where the time goes in v1:
time: 228 us
  blocking collectives  90.6 us (40%)
  Pallas kernels  62.8 us (28%)
  waiting for transfers between devices  40.5 us (18%)
  starting transfers between devices  24.6 us (11%)
  local copies, waits for them, and re-layouts  7.12 us (3%)
    all_to_all x4, blocking collectives, exchanged(): return lax.all_to_all(array, axis, 0, 0, tiled=True)  90.6 us
    pallas_call x1, Pallas kernels, direction_sums(): pl.pallas_call(kernel, out_shape=[jax.ShapeDtypeStruct((owners, 128, 128)...  44.8 us
    all_to_all x1, waiting for transfers between devices, exchanged(): return lax.all_to_all(array, axis, 0, 0, tiled=True)  38.3 us
    pallas_call x1, Pallas kernels, pack(): pl.pallas_call(pack_kernel, out_shape=[jax.ShapeDtypeStruct((56, 4, 8, 12...  11.6 us
    all_to_all x1, starting transfers between devices, exchanged(): return lax.all_to_all(array, axis, 0, 0, tiled=True)  10.3 us
    ppermute x1, starting transfers between devices, per_device(): got = lax.ppermute(send, 'row', swap)  7.08 us
    pallas_call x3, Pallas kernels, simple(): pl.pallas_call(kernel, out_shape=out_shape, in_specs=vmem(len(arrays)), o...  6.36 us
    unnamed x8, local copies, waits for them, and re-layouts  5.38 us
  transfers between devices with their start and end apart: 4, of which 3 were waited for; matrix products, arithmetic and copies ran while one was open for 1% of the time, Pallas kernels for 0%

profile of v1, /device:TPU:1, one launch (start us, length us, event | category | flops | bytes accessed | tf_op | source)
XLA Modules:
  0.0 227.8 jit_solution(4114125060834773721)
XLA Ops:
  0.6 1.7 copy.8.codes_ref
  2.4 1.7 copy.9.bins_ref
  4.1 11.6 %pack.1 = (f32[56,4,8,128]{3,2,1,0:T(8,128)}, s32[56,8,128]{2,1,0:T(8,128)}) custom-call(bf16[448,512]{1,0:T(8,128)(2,1)} %weights_ref.1, s32[448,64]{1,0:T(8,128)} %copy.8.codes_ref, s32[448,64]{1,0:T(8,128)} %copy.9.bins_ref), custom_call_target="tpu_custom_call" | custom-call | tf_op jit(solution)/shard_map/pack/pallas_call | solution.py:68
  15.7 1.0 copy.12
  16.9 29.3 %all_to_all.25 = s32[16,32,128]{2,1,0:T(8,128)S(1)} all-to-all(s32[16,32,128]{2,1,0:T(8,128)S(1)} %pad_add_fusion), channel_id=1, replica_groups=mesh['width'=16,'cb'=16,'row'=2] {'width'}, dimensions={0} | all-to-all | bytes 524288 | tf_op jit(solution)/shard_map/all_to_all | solution.py:253
  46.2 10.3 %all-to-all-start.1 = ((f32[16,14,8,128]{3,2,1,0:T(8,128)}), f32[16,14,8,128]{3,2,1,0:T(8,128)S(1)}, u32[]{:S(2)}, u32[]{:S(2)}) async-start(f32[16,14,8,128]{3,2,1,0:T(8,128)} %bitcast.3), calls=%async_computation.1 | async-start | bytes 1835008 | tf_op jit(solution)/shard_map/all_to_all | solution.py:253
  56.5 0.7 fusion
  57.2 0.7 reshape.29.refs_1_
  57.9 38.3 %all-to-all-done.1.refs_2_ = f32[16,14,8,128]{3,2,1,0:T(8,128)S(1)} async-done(((f32[16,14,8,128]{3,2,1,0:T(8,128)}), f32[16,14,8,128]{3,2,1,0:T(8,128)S(1)}, u32[]{:S(2)}, u32[]{:S(2)}) %all-to-all-start.1) | async-done | bytes 917536 | tf_op jit(solution)/shard_map/all_to_all | solution.py:253
  96.2 0.0 copy-start.1
  96.2 0.9 copy-done.1
  97.1 44.8 %sums.1 = (f32[16,128,128]{2,1,0:T(8,128)}, f32[16,128,128]{2,1,0:T(8,128)}, f32[8,128]{1,0:T(8,128)}) custom-call(s32[1]{0:T(128)} %bitcast.refs_0_, s32[28672]{0:T(1024)} %reshape.29.refs_1_, f32[16,14,8,128]{3,2,1,0:T(8,128)} %copy-done.1, s32[16,14,128]{2,1,0:T(8,128)} %get-tuple-element.18.refs_3_, s32[16,14,128]{2,1,0:T(8,128)} %get-tuple-element.16.refs_4_), custom_call_target="tpu_custom_call" | custom-call | flops 1000000000 | bytes 40000000 | tf_op jit(solution)/shard_map/sums/pallas_call | solution.py:198
  142.0 7.1 %collective-permute-start = (f32[16,128,128]{2,1,0:T(8,128)}, f32[16,128,128]{2,1,0:T(8,128)S(1)}, u32[]{:S(2)}, u32[]{:S(2)}) collective-permute-start(f32[16,128,128]{2,1,0:T(8,128)} %get-tuple-element.12), channel_id=1, source_target_pairs={{0,1},{1,0},{2,3},{3,2},{4,5},{5,4},{6,7},{7,6},{8,9},{9,8},{10,11... | collective-permute-start | bytes 3145736 | tf_op jit(solution)/shard_map/ppermute | solution.py:276
  149.1 1.9 collective-permute-start.1
  151.0 1.3 collective-permute-done.1.other_ref
  152.3 0.0 copy-start.2
  152.3 0.0 collective-permute-done.got_ref
  152.3 0.0 copy-start
  152.4 0.6 copy-done.2
  152.9 0.4 copy-done
  153.3 2.7 %join.1 = f32[16,136,128]{2,1,0:T(8,128)} custom-call(f32[16,128,128]{2,1,0:T(8,128)} %get-tuple-element.11.keep_ref, f32[16,128,128]{2,1,0:T(8,128)} %copy-done, f32[8,128]{1,0:T(8,128)} %get-tuple-element.13.totals_ref, f32[8,128]{1,0:T(8,128)} %copy-done.2), custom_call_target="tpu_custom_call" | custom-call | tf_op jit(solution)/shard_map/join/pallas_call | solution.py:247
  156.0 24.2 %all_to_all.26.parts_ref = f32[16,136,128]{2,1,0:T(8,128)} all-to-all(f32[16,136,128]{2,1,0:T(8,128)} %join.1), channel_id=1, replica_groups=mesh['width'=16,'cb'=16,'row'=2] {'cb'}, dimensions={0} | all-to-all | bytes 2228224 | tf_op jit(solution)/shard_map/all_to_all | solution.py:253
  180.2 2.0 owned.1
  182.1 20.1 %all_to_all.27.parts_ref = f32[16,16,128]{2,1,0:T(8,128)} all-to-all(f32[16,16,128]{2,1,0:T(8,128)} %owned.1), channel_id=1, replica_groups=mesh['width'=16,'cb'=16,'row'=2] {'width'}, dimensions={0} | all-to-all | bytes 262144 | tf_op jit(solution)/shard_map/all_to_all | solution.py:253
  202.3 1.7 finish.1
  204.0 17.0 %all_to_all.28 = f32[16,8,128]{2,1,0:T(8,128)S(1)} all-to-all(f32[16,8,128]{2,1,0:T(8,128)} %get-tuple-element.14), channel_id=1, replica_groups=mesh['width'=16,'cb'=16,'row'=2] {'width'}, dimensions={0} | all-to-all | bytes 131072 | tf_op jit(solution)/shard_map/all_to_all | solution.py:253
  220.9 5.2 %collective-permute-start.2 = (f32[128,128]{1,0:T(8,128)S(1)}, f32[128,128]{1,0:T(8,128)S(1)}, u32[]{:S(2)}, u32[]{:S(2)}) collective-permute-start(f32[128,128]{1,0:T(8,128)S(1)} %bitcast.11), channel_id=1, source_target_pairs={{0,1},{1,0},{2,3},{3,2},{4,5},{5,4},{6,7},{7,6},{8,9},{9,8},{10,11... | collective-permute-start | bytes 196616 | tf_op jit(solution)/shard_map/ppermute | solution.py:284
  226.2 0.9 collective-permute-done.2
  227.1 0.7 pad_maximum_fusion
  (6 shorter events, 0.2 us)
Async XLA Ops:
  46.2 50.0 %all-to-all-start.1 = ((f32[16,14,8,128]{3,2,1,0:T(8,128)}), f32[16,14,8,128]{3,2,1,0:T(8,128)S(1)}, u32[]{:S(2)}, u32[]{:S(2)}) async-start(f32[16,14,8,128]{3,2,1,0:T(8,128)} %bitcast.3), calls=%async_computation.1 | async-start | bytes 1835008 | tf_op jit(solution)/shard_map/all_to_all | solution.py:253
  96.2 0.9 copy-start.1
  142.0 10.4 %collective-permute-start = (f32[16,128,128]{2,1,0:T(8,128)}, f32[16,128,128]{2,1,0:T(8,128)S(1)}, u32[]{:S(2)}, u32[]{:S(2)}) collective-permute-start(f32[16,128,128]{2,1,0:T(8,128)} %get-tuple-element.12), channel_id=1, source_target_pairs={{0,1},{1,0},{2,3},{3,2},{4,5},{5,4},{6,7},{7,6},{8,9},{9,8},{10,11... | collective-permute-start | bytes 3145736 | tf_op jit(solution)/shard_map/ppermute | solution.py:276
  149.1 3.3 %collective-permute-start.1 = (f32[8,128]{1,0:T(8,128)}, f32[8,128]{1,0:T(8,128)S(1)}, u32[]{:S(2)}, u32[]{:S(2)}) collective-permute-start(f32[8,128]{1,0:T(8,128)} %get-tuple-element.13.totals_ref), channel_id=1, source_target_pairs={{0,1},{1,0},{2,3},{3,2},{4,5},{5,4},{6,7},{7,6},{8,9},{9,8},{10,11... | collective-permute-start | bytes 12296 | tf_op jit(solution)/shard_map/ppermute | solution.py:277
  152.3 0.6 copy-start.2
  152.3 1.0 copy-start
  220.9 6.1 %collective-permute-start.2 = (f32[128,128]{1,0:T(8,128)S(1)}, f32[128,128]{1,0:T(8,128)S(1)}, u32[]{:S(2)}, u32[]{:S(2)}) collective-permute-start(f32[128,128]{1,0:T(8,128)S(1)} %bitcast.11), channel_id=1, source_target_pairs={{0,1},{1,0},{2,3},{3,2},{4,5},{5,4},{6,7},{7,6},{8,9},{9,8},{10,11... | collective-permute-start | bytes 196616 | tf_op jit(solution)/shard_map/ppermute | solution.py:284

commit v2 on v1

v2 whole, which is shorter than its diff:
```python
import functools
import math

import jax
import jax.numpy as jnp
from jax import lax
from jax.experimental import pallas as pl
from jax.experimental.pallas import tpu as pltpu
from jax.sharding import PartitionSpec as P

WIDTH = 8192
CODES = 65536
NBINS = 256
SCALING = 1.0 / math.sqrt(WIDTH)
F32 = jnp.float32
I32 = jnp.int32

NEAR = 4
FAR = 4
SOURCES = NEAR * FAR
TILES = 14
CHUNKS = (8, 6)
ACCS = 8
CODE_ROWS = CODES // 16


def iota(shape, axis):
    return lax.broadcasted_iota(I32, shape, axis)


def lanes_at(values, index):
    return jnp.take_along_axis(values, index, axis=1, mode="promise_in_bounds")


def vmem(count):
    return [pl.BlockSpec(memory_space=pltpu.VMEM)] * count


def chunk_rows(tiles):
    return -(-10 * tiles // 8) * 8


def pack_kernel(wanted, weights_ref, codes_ref, bins_ref, out, lists_ref):
    common = jnp.bitwise_and(iota((128, 128), 0), iota((128, 128), 1))
    for shift in (4, 2, 1):
        common = jnp.bitwise_xor(common, common >> shift)
    hadamard = (1 - 2 * jnp.bitwise_and(common, 1)).astype(F32).astype(jnp.bfloat16)
    blocks = [
        jnp.dot(weights_ref[:, 128 * b : 128 * b + 128], hadamard, preferred_element_type=F32)
        for b in range(4)
    ]
    sums = [blocks[0] + blocks[1], blocks[0] - blocks[1], blocks[2] + blocks[3], blocks[2] - blocks[3]]
    blocks = [sums[0] + sums[2], sums[1] + sums[3], sums[0] - sums[2], sums[1] - sums[3]]
    lists_ref[:64, :448] = codes_ref[...].astype(F32)
    lists_ref[64:, :448] = bins_ref[...].astype(F32)
    lists = [lists_ref[:, 128 * i : 128 * i + 128].T for i in range(4)]
    lane = iota((8, 128), 1)
    own = jnp.bitwise_and(lane, 7) == iota((8, 128), 0)

    def spread(tile, column):
        block = lists[tile // 16][8 * (tile % 16) : 8 * (tile % 16) + 8, :]
        taken = lanes_at(block, column + (lane >> 3))
        return jnp.sum(jnp.where(own, taken, 0.0), axis=0, keepdims=True)

    for tile in range(56):
        for b in range(4):
            target, t = divmod(4 * tile + b, TILES)
            chunk = 0
            while t >= CHUNKS[chunk]:
                t -= CHUNKS[chunk]
                chunk += 1
            if chunk != wanted:
                continue
            tiles = CHUNKS[chunk]
            out[target, 8 * t : 8 * t + 8, :] = blocks[b][8 * tile : 8 * tile + 8, :]
            out[target, 8 * tiles + t : 8 * tiles + t + 1, :] = spread(tile, 16 * b)
            out[target, 9 * tiles + t : 9 * tiles + t + 1, :] = spread(tile, 64 + 16 * b)


def pack(wanted, weights, codes, bins):
    return pl.pallas_call(
        functools.partial(pack_kernel, wanted),
        out_shape=jax.ShapeDtypeStruct((SOURCES, chunk_rows(CHUNKS[wanted]), 128), F32),
        in_specs=vmem(3),
        out_specs=pl.BlockSpec(memory_space=pltpu.VMEM),
        cost_estimate=pl.CostEstimate(flops=10**9, bytes_accessed=2 * 10**6, transcendentals=0),
        scratch_shapes=[pltpu.VMEM((128, 512), F32)],
        name="pack",
    )(weights, codes, bins)


def sums_kernel(tiles, first, *refs):
    side_ref, parts_ref = refs[:2]
    before = refs[2:4] if not first else (None, None)
    keep_ref, send_ref, at_ref, at_sem, codes_ref, directions_ref = refs[-8 - ACCS : -2 - ACCS]
    items, accs = refs[-2 - ACCS : -ACCS], refs[-ACCS:]
    lane = iota((8, 128), 1)
    place = iota((8, 128), 0)
    inner = jnp.bitwise_and(lane, 7)
    outer = lane >> 3
    for h in range(SOURCES):
        codes_ref[h * tiles : (h + 1) * tiles, :] = parts_ref[h, 8 * tiles : 9 * tiles, :].astype(I32) >> 4
    fetch = pltpu.make_async_copy(codes_ref, at_ref, at_sem)
    fetch.start()
    for acc in accs:
        acc[...] = jnp.zeros_like(acc)
    group = (iota((128, 128), 0) >> 3 == iota((128, 128), 1) >> 3).astype(F32)

    def rotate(t, carry):
        z = [parts_ref[h, pl.ds(pl.multiple_of(8 * t, 8), 8), :] for h in range(SOURCES)]
        for bit in range(4):
            d = 1 << bit
            z = [z[h ^ d] - z[h] if h & d else z[h] + z[h ^ d] for h in range(SOURCES)]
        rotated = jnp.concatenate(z, axis=0) * SCALING
        squares = jnp.dot(
            rotated * rotated, group, precision=lax.Precision.HIGHEST, preferred_element_type=F32
        )
        floored = jnp.maximum(jnp.sqrt(squares), 1.0)
        directions = rotated / floored
        logs = jnp.log(floored)
        packed = []
        for half in range(2):
            log_sum = jnp.zeros((8, 128), F32)
            bin_sum = jnp.zeros((8, 128), I32)
            for j in range(8):
                h = 8 * half + j
                bins = jnp.broadcast_to(parts_ref[h, pl.ds(9 * tiles + t, 1), :], (8, 128)).astype(I32)
                bins = lanes_at(bins, 8 * outer + place)
                log_sum = log_sum + jnp.where(inner == j, logs[8 * h : 8 * h + 8], 0.0)
                bin_sum = bin_sum + jnp.where(inner == j, bins, 0)
            packed.append((log_sum, bin_sum))
        for h in range(SOURCES):
            directions_ref[h * tiles + t] = directions[8 * h : 8 * h + 8]
        base = packed[0][1] >> 4
        low, high, low_count, high_count = carry
        for offset in range(16):
            log_total = jnp.zeros((8, 128), F32)
            count = jnp.zeros((8, 128), F32)
            for log_sum, bin_sum in packed:
                chosen = jnp.bitwise_and(bin_sum, 15) == offset
                log_total = log_total + jnp.where(chosen, log_sum, 0.0)
                count = count + jnp.where(chosen, 1.0, 0.0)
            log_total = jnp.sum(log_total, axis=1, keepdims=True)
            count = jnp.sum(count, axis=1, keepdims=True)
            target = 16 * base + offset
            at_low, at_high = target == lane, target == lane + 128
            low = low + jnp.where(at_low, log_total, 0.0)
            high = high + jnp.where(at_high, log_total, 0.0)
            low_count = low_count + jnp.where(at_low, count, 0.0)
            high_count = high_count + jnp.where(at_high, count, 0.0)
        return low, high, low_count, high_count

    empty = jnp.zeros((8, 128), F32)
    bin_parts = lax.fori_loop(0, tiles, rotate, (empty,) * 4)
    rows = [jnp.sum(part, axis=0, keepdims=True) for part in bin_parts]
    totals = jnp.concatenate(rows + [jnp.zeros((4, 128), F32)], axis=0)

    def lay_out(n, items_ref):
        h, t = n // tiles, n % tiles
        direction = directions_ref[n]
        codes = jnp.broadcast_to(parts_ref[h, pl.ds(8 * tiles + t, 1), :], (8, 128)).astype(I32)
        codes = jnp.bitwise_and(codes, 15)
        for k in range(16):
            values = lanes_at(direction, 8 * k + inner)
            slot = lanes_at(codes, 8 * k + place)
            items_ref[8 * k : 8 * k + 8, :] = jnp.where(slot == outer, values, 0.0)

    def add(n, items_ref):
        for k in range(16):
            at = [at_ref[n, 8 * k + s] for s in range(ACCS)]
            old = [accs[s][pl.ds(at[s], 1), :] for s in range(ACCS)]
            for s in range(ACCS):
                accs[s][pl.ds(at[s], 1), :] = old[s] + items_ref[8 * k + s : 8 * k + s + 1, :]

    count = SOURCES * tiles
    fetch.wait()
    lay_out(0, items[0])

    def step(i, carry):
        n = 2 * i
        lay_out(n + 1, items[1])
        add(n, items[0])
        lay_out(jnp.minimum(n + 2, count - 1), items[0])
        add(n + 1, items[1])
        return carry

    lax.fori_loop(0, count // 2, step, 0)
    side = side_ref[0]

    def finish(c, carry):
        for ref, earlier, mine in ((keep_ref, before[0], side), (send_ref, before[1], 1 - side)):
            for near in range(NEAR):
                start = pl.multiple_of(c * 256 + near * 64 + mine * 32, 32)
                total = accs[0][pl.ds(start, 32), :]
                for acc in accs[1:]:
                    total = total + acc[pl.ds(start, 32), :]
                rows = slice(32 * near, 32 * near + 32)
                ref[c, rows] = total if first else total + earlier[c, rows]
            ref[c, 128:] = totals if first else totals + earlier[c, 128:]
        return carry

    lax.fori_loop(0, CODE_ROWS // 256, finish, 0)


def direction_sums(side, parts, tiles, before):
    owners = CODE_ROWS // 256
    arrays = () if before is None else tuple(before)

    def kernel(*refs):
        sums_kernel(tiles, before is None, *refs)

    return pl.pallas_call(
        kernel,
        out_shape=[jax.ShapeDtypeStruct((owners, 136, 128), F32)] * 2,
        in_specs=[pl.BlockSpec(memory_space=pltpu.SMEM)] + vmem(1 + len(arrays)),
        out_specs=vmem(2),
        scratch_shapes=[
            pltpu.SMEM((SOURCES * tiles, 128), I32),
            pltpu.SemaphoreType.DMA,
            pltpu.VMEM((SOURCES * tiles, 128), I32),
            pltpu.VMEM((SOURCES * tiles, 8, 128), F32),
        ]
        + [pltpu.VMEM((128, 128), F32)] * 2
        + [pltpu.VMEM((CODE_ROWS, 128), F32)] * ACCS,
        cost_estimate=pl.CostEstimate(
            flops=2 * 10**9 * tiles, bytes_accessed=4 * 10**6 * tiles, transcendentals=0
        ),
        name="sums",
    )(side, parts, *arrays)


def summed(parts_ref):
    total = parts_ref[0]
    for i in range(1, parts_ref.shape[0]):
        total = total + parts_ref[i]
    return total


def owned_kernel(parts_ref, out_ref):
    total = summed(parts_ref)
    for near in range(NEAR):
        out_ref[near, :32] = total[32 * near : 32 * near + 32]
        out_ref[near, 32:] = total[128:]


def spread_kernel(parts_ref, out_ref):
    out_ref[...] = jnp.broadcast_to(summed(parts_ref)[None], out_ref.shape)


def finish_kernel(parts_ref, words_ref, levels_ref):
    total = summed(parts_ref)
    sums = total[:32]
    group = (iota((128, 128), 0) >> 3 == iota((128, 128), 1) >> 3).astype(F32)
    squares = jnp.dot(sums * sums, group, precision=lax.Precision.HIGHEST, preferred_element_type=F32)
    words = sums / jnp.maximum(jnp.sqrt(squares), 1.0)
    words_ref[...] = jnp.broadcast_to(words[None], words_ref.shape)
    levels_ref[...] = total[32:34] / jnp.maximum(total[34:36], 1.0)


def simple(kernel, name, shapes, *arrays):
    out_shape = [jax.ShapeDtypeStruct(shape, F32) for shape in shapes]
    return pl.pallas_call(
        kernel, out_shape=out_shape, in_specs=vmem(len(arrays)), out_specs=vmem(len(shapes)), name=name
    )(*arrays)


def exchanged(array, axis):
    return lax.all_to_all(array, axis, 0, 0, tiled=True)


def per_device(weights, dir_codes, norm_bins):
    side = lax.axis_index("row")
    received = [
        exchanged(pack(chunk, weights, dir_codes.T, norm_bins.T), ("far", "near"))
        for chunk in range(len(CHUNKS))
    ]
    sums = None
    for chunk, tiles in zip(received, CHUNKS):
        sums = direction_sums(side.reshape(1), chunk, tiles, sums)
    keep, send = sums
    joined = exchanged(keep + lax.ppermute(send, "row", [(0, 1), (1, 0)]), "cb")
    (owned,) = simple(owned_kernel, "owned", [(NEAR, 40, 128)], joined)
    (owned,) = simple(spread_kernel, "spread", [(FAR, 40, 128)], exchanged(owned, "near"))
    words, levels = simple(
        finish_kernel, "finish", [(2 * NEAR, 32, 128), (2, 128)], exchanged(owned, "far")
    )
    codewords = exchanged(words, ("near", "row"))
    return codewords.reshape(256, 128), levels.reshape(NBINS)


def solution(mesh):
    names = {"width": ("far", "near"), "cb": ("cb",), "row": ("row",)}
    sizes = {"far": FAR, "near": NEAR, "cb": mesh.shape["cb"], "row": mesh.shape["row"]}
    axes = tuple(part for name in mesh.axis_names for part in names[name])
    fine = jax.sharding.Mesh(mesh.devices.reshape([sizes[axis] for axis in axes]), axes)
    spec = P(("cb", "row"), ("far", "near"))
    return jax.shard_map(
        per_device,
        mesh=fine,
        in_specs=(spec,) * 3,
        out_specs=(P("cb", None), P()),
        check_vma=False,
    )
```

time: 228 us -> 193 us (0.85)
  blocking collectives: 90.6 us -> 66.7 us
  waiting for transfers between devices: 40.5 us -> 28.8 us
  starting transfers between devices: 24.6 us -> 33.2 us
  local copies, waits for them, and re-layouts: 7.12 us -> 1.45 us
  Pallas kernels: 62.8 us -> 59.4 us
    all_to_all x4, blocking collectives: 90.6 us -> 66.7 us  [exchanged(): return lax.all_to_all(array, axis, 0, 0, tiled=True)]
    all_to_all x1 -> x2, starting transfers between devices: 10.3 us -> 28 us  [exchanged(): return lax.all_to_all(array, axis, 0, 0, tiled=True)]
    all_to_all x1 -> x2, waiting for transfers between devices: 38.3 us -> 26.3 us  [exchanged(): return lax.all_to_all(array, axis, 0, 0, tiled=True)]
    ppermute x3 -> x1, starting transfers between devices: 14.2 us -> 5.28 us  [per_device(): joined = exchanged(keep + lax.ppermute(send, 'row', [(0, 1), (1, 0)]), 'cb')]
    unnamed x8 -> x5, local copies, waits for them, and re-layouts: 5.38 us -> 1.45 us
    pallas_call x2 -> x4, Pallas kernels: 56.5 us -> 54.2 us  [the longest x2 48.7 us: direction_sums(): pl.pallas_call(kernel, out_shape=[jax.ShapeDtypeStruct((owners, 136, 128)...]
  transfers between devices with their start and end apart: 4 -> 3, of which waited for: 3 -> 2; matrix products, arithmetic and copies ran while one was open for 1% -> 0% of each run, Pallas kernels for 0% -> 15%
where the time goes in v2:
time: 193 us; the launch traced here: 192 us
  blocking collectives  66.7 us (35%)
  Pallas kernels  59.4 us (31%)
  starting transfers between devices  33.2 us (17%)
  waiting for transfers between devices  28.8 us (15%)
    all_to_all x4, blocking collectives, exchanged(): return lax.all_to_all(array, axis, 0, 0, tiled=True)  66.7 us
    pallas_call x2, Pallas kernels, direction_sums(): pl.pallas_call(kernel, out_shape=[jax.ShapeDtypeStruct((owners, 136, 128)...  48.7 us
    all_to_all x2, starting transfers between devices, exchanged(): return lax.all_to_all(array, axis, 0, 0, tiled=True)  28 us
    all_to_all x2, waiting for transfers between devices, exchanged(): return lax.all_to_all(array, axis, 0, 0, tiled=True)  26.3 us
    pallas_call x2, Pallas kernels, pack(): pl.pallas_call(functools.partial(pack_kernel, wanted), out_shape=jax.Shap...  5.5 us
    ppermute x1, starting transfers between devices, per_device(): joined = exchanged(keep + lax.ppermute(send, 'row', [(0, 1), (1, 0)]), 'cb')  5.28 us
    pallas_call x3, Pallas kernels, simple(): pl.pallas_call(kernel, out_shape=out_shape, in_specs=vmem(len(arrays)), o...  5.2 us
  transfers between devices with their start and end apart: 3, of which 2 were waited for; matrix products, arithmetic and copies ran while one was open for 0% of the time, Pallas kernels for 15%

profile of v2, /device:TPU:1, one launch (start us, length us, event | category | flops | bytes accessed | tf_op | source)
XLA Modules:
  0.0 191.7 jit_solution(10939305571826250687)
XLA Ops:
  0.6 2.9 %pack.3 = f32[16,80,128]{2,1,0:T(8,128)} custom-call(bf16[448,512]{1,0:T(8,128)(2,1)} %weights_ref.3, s32[64,448]{1,0:T(8,128)} %bitcast.6, s32[64,448]{1,0:T(8,128)} %bitcast.8), custom_call_target="tpu_custom_call" | custom-call | flops 1000000000 | bytes 2000000 | tf_op jit(solution)/shard_map/pack/pallas_call | solution.py:81
  3.5 15.7 %all-to-all-start.1 = ((f32[16,80,128]{2,1,0:T(8,128)}), f32[16,80,128]{2,1,0:T(8,128)S(1)}, u32[]{:S(2)}, u32[]{:S(2)}) async-start(f32[16,80,128]{2,1,0:T(8,128)} %pack.3), calls=%async_computation.1 | async-start | bytes 1310720 | tf_op jit(solution)/shard_map/all_to_all | solution.py:268
  19.2 2.6 %pack.2 = f32[16,64,128]{2,1,0:T(8,128)} custom-call(bf16[448,512]{1,0:T(8,128)(2,1)} %weights_ref.3, s32[64,448]{1,0:T(8,128)} %bitcast.7, s32[64,448]{1,0:T(8,128)} %bitcast.9), custom_call_target="tpu_custom_call" | custom-call | flops 1000000000 | bytes 2000000 | tf_op jit(solution)/shard_map/pack/pallas_call | solution.py:81
  21.9 26.3 %all-to-all-done.1.refs_1_ = f32[16,80,128]{2,1,0:T(8,128)S(1)} async-done(((f32[16,80,128]{2,1,0:T(8,128)}), f32[16,80,128]{2,1,0:T(8,128)S(1)}, u32[]{:S(2)}, u32[]{:S(2)}) %all-to-all-start.1) | async-done | bytes 655392 | tf_op jit(solution)/shard_map/all_to_all | solution.py:268
  48.1 0.0 copy-start
  48.1 12.2 %all-to-all-start = ((f32[16,64,128]{2,1,0:T(8,128)}), f32[16,64,128]{2,1,0:T(8,128)S(1)}, u32[]{:S(2)}, u32[]{:S(2)}) async-start(f32[16,64,128]{2,1,0:T(8,128)} %pack.2), calls=%async_computation | async-start | bytes 1048576 | tf_op jit(solution)/shard_map/all_to_all | solution.py:268
  60.4 0.0 copy-done
  60.4 26.6 %sums.2 = (f32[16,136,128]{2,1,0:T(8,128)}, f32[16,136,128]{2,1,0:T(8,128)}) custom-call(s32[1]{0:T(128)} %bitcast.refs_0_, f32[16,80,128]{2,1,0:T(8,128)} %copy-done), custom_call_target="tpu_custom_call" | custom-call | flops 16000000000 | bytes 32000000 | tf_op jit(solution)/shard_map/sums/pallas_call | solution.py:212
  86.9 0.0 all-to-all-done.refs_1_
  87.0 0.0 copy-start.1
  87.0 0.8 copy-done.1
  87.8 22.1 %sums.3 = (f32[16,136,128]{2,1,0:T(8,128)}, f32[16,136,128]{2,1,0:T(8,128)}) custom-call(s32[1]{0:T(128)} %bitcast.refs_0_, f32[16,64,128]{2,1,0:T(8,128)} %copy-done.1, f32[16,136,128]{2,1,0:T(8,128)} %get-tuple-element.8.refs_2_, f32[16,136,128]{2,1,0:T(8,128)} %get-tuple-element.9.refs_3_), custom_call_target="tpu_custom_call" | custom-call | flops 12000000000 | bytes 24000000 | tf_op jit(solution)/shard_map/sums/pallas_call | solution.py:212
  109.9 5.3 %collective-permute-start = (f32[16,136,128]{2,1,0:T(8,128)}, f32[16,136,128]{2,1,0:T(8,128)S(1)}, u32[]{:S(2)}, u32[]{:S(2)}) collective-permute-start(f32[16,136,128]{2,1,0:T(8,128)} %get-tuple-element.11), channel_id=1, source_target_pairs={{0,1},{1,0},{2,3},{3,2},{4,5},{5,4},{6,7},{7,6},{8,9},{9,8},{10,11... | collective-permute-start | bytes 3342344 | tf_op jit(solution)/shard_map/ppermute | solution.py:281
  115.2 2.6 %collective-permute-done = f32[16,136,128]{2,1,0:T(8,128)S(1)} collective-permute-done((f32[16,136,128]{2,1,0:T(8,128)}, f32[16,136,128]{2,1,0:T(8,128)S(1)}, u32[]{:S(2)}, u32[]{:S(2)}) %collective-permute-start) | collective-permute-done | bytes 1114144 | tf_op jit(solution)/shard_map/ppermute | solution.py:281
  117.7 1.4 add.3
  119.1 23.8 %all_to_all.30.parts_ref = f32[16,136,128]{2,1,0:T(8,128)} all-to-all(f32[16,136,128]{2,1,0:T(8,128)S(1)} %add.3), channel_id=1, replica_groups=mesh['far'=4,'near'=4,'cb'=16,'row'=2] {'cb'}, dimensions={0} | all-to-all | bytes 2228224 | tf_op jit(solution)/shard_map/all_to_all | solution.py:268
  142.9 1.9 %owned.1 = f32[4,40,128]{2,1,0:T(8,128)} custom-call(f32[16,136,128]{2,1,0:T(8,128)} %all_to_all.30.parts_ref), custom_call_target="tpu_custom_call" | custom-call | tf_op jit(solution)/shard_map/owned/pallas_call | solution.py:262
  144.9 8.8 %all_to_all.31.parts_ref = f32[4,40,128]{2,1,0:T(8,128)} all-to-all(f32[4,40,128]{2,1,0:T(8,128)} %owned.1), channel_id=1, replica_groups=mesh['far'=4,'near'=4,'cb'=16,'row'=2] {'near'}, dimensions={0} | all-to-all | bytes 163840 | tf_op jit(solution)/shard_map/all_to_all | solution.py:268
  153.7 1.5 spread.1
  155.2 20.8 %all_to_all.32.parts_ref = f32[4,40,128]{2,1,0:T(8,128)} all-to-all(f32[4,40,128]{2,1,0:T(8,128)} %spread.1), channel_id=1, replica_groups=mesh['far'=4,'near'=4,'cb'=16,'row'=2] {'far'}, dimensions={0} | all-to-all | bytes 163840 | tf_op jit(solution)/shard_map/all_to_all | solution.py:268
  176.0 1.7 finish.1
  177.7 13.3 %all_to_all.33 = f32[8,32,128]{2,1,0:T(8,128)S(1)} all-to-all(f32[8,32,128]{2,1,0:T(8,128)} %get-tuple-element.12), channel_id=1, replica_groups=mesh['far'=4,'near'=4,'cb'=16,'row'=2] {'near','row'}, dimensions={0} | all-to-all | bytes 262144 | tf_op jit(solution)/shard_map/all_to_all | solution.py:268
  191.0 0.7 copy.6
Async XLA Ops:
  3.5 44.6 %all-to-all-start.1 = ((f32[16,80,128]{2,1,0:T(8,128)}), f32[16,80,128]{2,1,0:T(8,128)S(1)}, u32[]{:S(2)}, u32[]{:S(2)}) async-start(f32[16,80,128]{2,1,0:T(8,128)} %pack.3), calls=%async_computation.1 | async-start | bytes 1310720 | tf_op jit(solution)/shard_map/all_to_all | solution.py:268
  48.1 12.2 %copy-start = (f32[16,80,128]{2,1,0:T(8,128)}, f32[16,80,128]{2,1,0:T(8,128)S(1)}, u32[]{:S(2)}) copy-start(f32[16,80,128]{2,1,0:T(8,128)S(1)} %all-to-all-done.1.refs_1_) | copy-start | bytes 1966084
  48.1 38.8 %all-to-all-start = ((f32[16,64,128]{2,1,0:T(8,128)}), f32[16,64,128]{2,1,0:T(8,128)S(1)}, u32[]{:S(2)}, u32[]{:S(2)}) async-start(f32[16,64,128]{2,1,0:T(8,128)} %pack.2), calls=%async_computation | async-start | bytes 1048576 | tf_op jit(solution)/shard_map/all_to_all | solution.py:268
  87.0 0.8 copy-start.1
  109.9 7.9 %collective-permute-start = (f32[16,136,128]{2,1,0:T(8,128)}, f32[16,136,128]{2,1,0:T(8,128)S(1)}, u32[]{:S(2)}, u32[]{:S(2)}) collective-permute-start(f32[16,136,128]{2,1,0:T(8,128)} %get-tuple-element.11), channel_id=1, source_target_pairs={{0,1},{1,0},{2,3},{3,2},{4,5},{5,4},{6,7},{7,6},{8,9},{9,8},{10,11... | collective-permute-start | bytes 3342344 | tf_op jit(solution)/shard_map/ppermute | solution.py:281

commit v3 on v2

--- a/solution.py
+++ b/solution.py
@@ -15,12 +15,15 @@
 F32 = jnp.float32
 I32 = jnp.int32
 
-NEAR = 4
-FAR = 4
+NEAR = 2
+FAR = 8
+PIECE = 128 // NEAR
 SOURCES = NEAR * FAR
 TILES = 14
 CHUNKS = (8, 6)
 ACCS = 8
+ITEMS = 4
+SCRATCH = 2 + 3 * ACCS + ITEMS
 CODE_ROWS = CODES // 16
 
 
@@ -91,20 +94,41 @@
 
 def sums_kernel(tiles, first, *refs):
     side_ref, parts_ref = refs[:2]
-    before = refs[2:4] if not first else (None, None)
-    keep_ref, send_ref, at_ref, at_sem, codes_ref, directions_ref = refs[-8 - ACCS : -2 - ACCS]
-    items, accs = refs[-2 - ACCS : -ACCS], refs[-ACCS:]
+    inputs = 2 if first else 4
+    keep_ref, send_ref = refs[inputs : inputs + 2]
+    scratch = refs[inputs + 2 : inputs + 2 + SCRATCH]
+    loads = []
+    before = refs[inputs + 2 + SCRATCH :]
+    if not first:
+        sums_sems, before = before[0], before[1:]
+        loads = [pltpu.make_async_copy(refs[2 + i], before[i], sums_sems.at[i]) for i in range(2)]
+        for load in loads:
+            load.start()
+    at_sems, directions_ref = scratch[0], scratch[1]
+    rows_refs, at_refs = scratch[2 : 2 + ACCS], scratch[2 + ACCS : 2 + 2 * ACCS]
+    accs, items = scratch[2 + 2 * ACCS : 2 + 3 * ACCS], scratch[2 + 3 * ACCS :]
     lane = iota((8, 128), 1)
     place = iota((8, 128), 0)
     inner = jnp.bitwise_and(lane, 7)
     outer = lane >> 3
-    for h in range(SOURCES):
-        codes_ref[h * tiles : (h + 1) * tiles, :] = parts_ref[h, 8 * tiles : 9 * tiles, :].astype(I32) >> 4
-    fetch = pltpu.make_async_copy(codes_ref, at_ref, at_sem)
-    fetch.start()
-    for acc in accs:
-        acc[...] = jnp.zeros_like(acc)
+    for t in range(tiles):
+        for h in range(SOURCES):
+            row = parts_ref[h, 8 * tiles + t : 8 * tiles + t + 1, :].astype(I32) >> 4
+            m = 2 * t + h // ACCS
+            rows_refs[h % ACCS][m : m + 1, :] = row
+    fetches = [
+        pltpu.make_async_copy(rows_refs[j], at_refs[j], at_sems.at[j]) for j in range(ACCS)
+    ]
+    for fetch in fetches:
+        fetch.start()
+    share = -(-CODE_ROWS // (8 * tiles))
     group = (iota((128, 128), 0) >> 3 == iota((128, 128), 1) >> 3).astype(F32)
+
+    def clear(t, offset):
+        start = jnp.minimum(t * share, CODE_ROWS // 8 - share)
+        for i in range(offset, share, 16):
+            for acc in accs:
+                acc[pl.ds(pl.multiple_of(8 * (start + i), 8), 8), :] = jnp.zeros((8, 128), F32)
 
     def rotate(t, carry):
         z = [parts_ref[h, pl.ds(pl.multiple_of(8 * t, 8), 8), :] for h in range(SOURCES)]
@@ -130,10 +154,11 @@
                 bin_sum = bin_sum + jnp.where(inner == j, bins, 0)
             packed.append((log_sum, bin_sum))
         for h in range(SOURCES):
-            directions_ref[h * tiles + t] = directions[8 * h : 8 * h + 8]
+            directions_ref[SOURCES * t + h] = directions[8 * h : 8 * h + 8]
         base = packed[0][1] >> 4
         low, high, low_count, high_count = carry
         for offset in range(16):
+            clear(t, offset)
             log_total = jnp.zeros((8, 128), F32)
             count = jnp.zeros((8, 128), F32)
             for log_sum, bin_sum in packed:
@@ -155,55 +180,53 @@
     rows = [jnp.sum(part, axis=0, keepdims=True) for part in bin_parts]
     totals = jnp.concatenate(rows + [jnp.zeros((4, 128), F32)], axis=0)
 
-    def lay_out(n, items_ref):
-        h, t = n // tiles, n % tiles
-        direction = directions_ref[n]
-        codes = jnp.broadcast_to(parts_ref[h, pl.ds(8 * tiles + t, 1), :], (8, 128)).astype(I32)
-        codes = jnp.bitwise_and(codes, 15)
+    for fetch in fetches:
+        fetch.wait()
+
+    def step(m, carry):
+        t, half = m >> 1, jnp.bitwise_and(m, 1)
+        moved = [directions_ref[ACCS * m + j] for j in range(ACCS)]
+        slots = []
+        for j in range(ACCS):
+            row = parts_ref[ACCS * half + j, pl.ds(8 * tiles + t, 1), :]
+            slots.append(jnp.bitwise_and(jnp.broadcast_to(row, (8, 128)).astype(I32), 15))
         for k in range(16):
-            values = lanes_at(direction, 8 * k + inner)
-            slot = lanes_at(codes, 8 * k + place)
-            items_ref[8 * k : 8 * k + 8, :] = jnp.where(slot == outer, values, 0.0)
-
-    def add(n, items_ref):
-        for k in range(16):
-            at = [at_ref[n, 8 * k + s] for s in range(ACCS)]
-            old = [accs[s][pl.ds(at[s], 1), :] for s in range(ACCS)]
-            for s in range(ACCS):
-                accs[s][pl.ds(at[s], 1), :] = old[s] + items_ref[8 * k + s : 8 * k + s + 1, :]
-
-    count = SOURCES * tiles
-    fetch.wait()
-    lay_out(0, items[0])
-
-    def step(i, carry):
-        n = 2 * i
-        lay_out(n + 1, items[1])
-        add(n, items[0])
-        lay_out(jnp.minimum(n + 2, count - 1), items[0])
-        add(n + 1, items[1])
+            items_ref = items[k % len(items)]
+            for j in range(ACCS):
+                values = lanes_at(moved[j], 8 * k + inner)
+                slot = lanes_at(slots[j], 8 * k + place)
+                items_ref[8 * j : 8 * j + 8, :] = jnp.where(slot == outer, values, 0.0)
+            for s in range(8):
+                at = [at_refs[j][m, 8 * k + s] for j in range(ACCS)]
+                old = [accs[j][pl.ds(at[j], 1), :] for j in range(ACCS)]
+                for j in range(ACCS):
+                    accs[j][pl.ds(at[j], 1), :] = old[j] + items_ref[8 * j + s : 8 * j + s + 1, :]
         return carry
 
-    lax.fori_loop(0, count // 2, step, 0)
+    lax.fori_loop(0, 2 * tiles, step, 0)
     side = side_ref[0]
 
+    owners = CODE_ROWS // 256
+    for load in loads:
+        load.wait()
+
     def finish(c, carry):
-        for ref, earlier, mine in ((keep_ref, before[0], side), (send_ref, before[1], 1 - side)):
+        for i, ref, mine in ((0, keep_ref, side), (1, send_ref, 1 - side)):
             for near in range(NEAR):
-                start = pl.multiple_of(c * 256 + near * 64 + mine * 32, 32)
-                total = accs[0][pl.ds(start, 32), :]
+                start = pl.multiple_of(c * 256 + (2 * near + mine) * PIECE, PIECE)
+                total = accs[0][pl.ds(start, PIECE), :]
                 for acc in accs[1:]:
-                    total = total + acc[pl.ds(start, 32), :]
-                rows = slice(32 * near, 32 * near + 32)
-                ref[c, rows] = total if first else total + earlier[c, rows]
-            ref[c, 128:] = totals if first else totals + earlier[c, 128:]
+                    total = total + acc[pl.ds(start, PIECE), :]
+                to = near * owners + c
+                ref[to, :PIECE] = total if first else total + before[i][to, :PIECE]
+                ref[to, PIECE:] = totals if first else totals + before[i][to, PIECE:]
         return carry
 
-    lax.fori_loop(0, CODE_ROWS // 256, finish, 0)
+    lax.fori_loop(0, owners, finish, 0)
 
 
 def direction_sums(side, parts, tiles, before):
-    owners = CODE_ROWS // 256
+    shape = (NEAR * CODE_ROWS // 256, PIECE + 8, 128)
     arrays = () if before is None else tuple(before)
 
     def kernel(*refs):
@@ -211,17 +234,20 @@
 
     return pl.pallas_call(
         kernel,
-        out_shape=[jax.ShapeDtypeStruct((owners, 136, 128), F32)] * 2,
-        in_specs=[pl.BlockSpec(memory_space=pltpu.SMEM)] + vmem(1 + len(arrays)),
+        out_shape=[jax.ShapeDtypeStruct(shape, F32)] * 2,
+        in_specs=[pl.BlockSpec(memory_space=pltpu.SMEM)]
+        + vmem(1)
+        + [pl.BlockSpec(memory_space=pl.ANY)] * len(arrays),
         out_specs=vmem(2),
         scratch_shapes=[
-            pltpu.SMEM((SOURCES * tiles, 128), I32),
-            pltpu.SemaphoreType.DMA,
-            pltpu.VMEM((SOURCES * tiles, 128), I32),
+            pltpu.SemaphoreType.DMA((ACCS,)),
             pltpu.VMEM((SOURCES * tiles, 8, 128), F32),
         ]
-        + [pltpu.VMEM((128, 128), F32)] * 2
-        + [pltpu.VMEM((CODE_ROWS, 128), F32)] * ACCS,
+        + [pltpu.VMEM((2 * tiles, 128), I32)] * ACCS
+        + [pltpu.SMEM((2 * tiles, 128), I32)] * ACCS
+        + [pltpu.VMEM((CODE_ROWS, 128), F32)] * ACCS
+        + [pltpu.VMEM((8 * ACCS, 128), F32)] * ITEMS
+        + ([] if before is None else [pltpu.SemaphoreType.DMA((2,))] + [pltpu.VMEM(shape, F32)] * 2),
         cost_estimate=pl.CostEstimate(
             flops=2 * 10**9 * tiles, bytes_accessed=4 * 10**6 * tiles, transcendentals=0
         ),
@@ -237,24 +263,17 @@
 
 
 def owned_kernel(parts_ref, out_ref):
-    total = summed(parts_ref)
-    for near in range(NEAR):
-        out_ref[near, :32] = total[32 * near : 32 * near + 32]
-        out_ref[near, 32:] = total[128:]
-
-
-def spread_kernel(parts_ref, out_ref):
     out_ref[...] = jnp.broadcast_to(summed(parts_ref)[None], out_ref.shape)
 
 
 def finish_kernel(parts_ref, words_ref, levels_ref):
     total = summed(parts_ref)
-    sums = total[:32]
+    sums = total[:PIECE]
     group = (iota((128, 128), 0) >> 3 == iota((128, 128), 1) >> 3).astype(F32)
     squares = jnp.dot(sums * sums, group, precision=lax.Precision.HIGHEST, preferred_element_type=F32)
     words = sums / jnp.maximum(jnp.sqrt(squares), 1.0)
     words_ref[...] = jnp.broadcast_to(words[None], words_ref.shape)
-    levels_ref[...] = total[32:34] / jnp.maximum(total[34:36], 1.0)
+    levels_ref[...] = total[PIECE : PIECE + 2] / jnp.maximum(total[PIECE + 2 : PIECE + 4], 1.0)
 
 
 def simple(kernel, name, shapes, *arrays):
@@ -278,11 +297,10 @@
     for chunk, tiles in zip(received, CHUNKS):
         sums = direction_sums(side.reshape(1), chunk, tiles, sums)
     keep, send = sums
-    joined = exchanged(keep + lax.ppermute(send, "row", [(0, 1), (1, 0)]), "cb")
-    (owned,) = simple(owned_kernel, "owned", [(NEAR, 40, 128)], joined)
-    (owned,) = simple(spread_kernel, "spread", [(FAR, 40, 128)], exchanged(owned, "near"))
+    joined = exchanged(keep + lax.ppermute(send, "row", [(0, 1), (1, 0)]), ("near", "cb"))
+    (owned,) = simple(owned_kernel, "owned", [(FAR, PIECE + 8, 128)], joined)
     words, levels = simple(
-        finish_kernel, "finish", [(2 * NEAR, 32, 128), (2, 128)], exchanged(owned, "far")
+        finish_kernel, "finish", [(2 * NEAR, PIECE, 128), (2, 128)], exchanged(owned, "far")
     )
     codewords = exchanged(words, ("near", "row"))
     return codewords.reshape(256, 128), levels.reshape(NBINS)

time: 193 us -> 184 us (0.953)
  Pallas kernels: 59.4 us -> 51.3 us
  blocking collectives: 66.7 us -> 63 us
  starting transfers between devices: 33.2 us -> 36.9 us
    pallas_call x2, Pallas kernels: 48.7 us -> 41.9 us  [direction_sums(): pl.pallas_call(kernel, out_shape=[jax.ShapeDtypeStruct(shape, F32)] * 2,...]
    all_to_all x4 -> x3, blocking collectives: 66.7 us -> 63 us  [exchanged(): return lax.all_to_all(array, axis, 0, 0, tiled=True)]
    ppermute x1, starting transfers between devices: 5.28 us -> 8.91 us  [per_device(): lax.ppermute(send, 'row', [(0, 1), (1, 0)])]
    pallas_call x3 -> x2, Pallas kernels: 5.2 us -> 3.9 us  [simple(): pl.pallas_call(kernel, out_shape=out_shape, in_specs=vmem(len(arrays)), o...]
  transfers between devices with their start and end apart: 3 -> 3, of which waited for: 2 -> 2; matrix products, arithmetic and copies ran while one was open for 0% -> 0% of each run, Pallas kernels for 15% -> 14%
where the time goes in v3:
time: 184 us
  blocking collectives  63 us (34%)
  Pallas kernels  51.3 us (28%)
  starting transfers between devices  36.9 us (20%)
  waiting for transfers between devices  28.9 us (16%)
    all_to_all x3, blocking collectives, exchanged(): return lax.all_to_all(array, axis, 0, 0, tiled=True)  63 us
    pallas_call x2, Pallas kernels, direction_sums(): pl.pallas_call(kernel, out_shape=[jax.ShapeDtypeStruct(shape, F32)] * 2,...  41.9 us
    all_to_all x2, starting transfers between devices, exchanged(): return lax.all_to_all(array, axis, 0, 0, tiled=True)  28 us
    all_to_all x2, waiting for transfers between devices, exchanged(): return lax.all_to_all(array, axis, 0, 0, tiled=True)  26.3 us
    ppermute x1, starting transfers between devices, per_device(): lax.ppermute(send, 'row', [(0, 1), (1, 0)])  8.91 us
    pallas_call x2, Pallas kernels, pack(): pl.pallas_call(functools.partial(pack_kernel, wanted), out_shape=jax.Shap...  5.49 us
    pallas_call x2, Pallas kernels, simple(): pl.pallas_call(kernel, out_shape=out_shape, in_specs=vmem(len(arrays)), o...  3.9 us
  transfers between devices with their start and end apart: 3, of which 2 were waited for; matrix products, arithmetic and copies ran while one was open for 0% of the time, Pallas kernels for 14%

profile of v3, /device:TPU:1, one launch (start us, length us, event | category | flops | bytes accessed | tf_op | source)
XLA Modules:
  0.0 183.6 jit_solution(3015008258091138723)
XLA Ops:
  0.6 2.9 %pack.3 = f32[16,80,128]{2,1,0:T(8,128)} custom-call(bf16[448,512]{1,0:T(8,128)(2,1)} %weights_ref.3, s32[64,448]{1,0:T(8,128)} %bitcast.6, s32[64,448]{1,0:T(8,128)} %bitcast.8), custom_call_target="tpu_custom_call" | custom-call | flops 1000000000 | bytes 2000000 | tf_op jit(solution)/shard_map/pack/pallas_call | solution.py:84
  3.5 15.7 %all-to-all-start.1 = ((f32[16,80,128]{2,1,0:T(8,128)}), f32[16,80,128]{2,1,0:T(8,128)S(1)}, u32[]{:S(2)}, u32[]{:S(2)}) async-start(f32[16,80,128]{2,1,0:T(8,128)} %pack.3), calls=%async_computation.1 | async-start | bytes 1310720 | tf_op jit(solution)/shard_map/all_to_all | solution.py:287
  19.2 2.6 %pack.2 = f32[16,64,128]{2,1,0:T(8,128)} custom-call(bf16[448,512]{1,0:T(8,128)(2,1)} %weights_ref.3, s32[64,448]{1,0:T(8,128)} %bitcast.7, s32[64,448]{1,0:T(8,128)} %bitcast.9), custom_call_target="tpu_custom_call" | custom-call | flops 1000000000 | bytes 2000000 | tf_op jit(solution)/shard_map/pack/pallas_call | solution.py:84
  21.9 26.3 %all-to-all-done.1.refs_1_ = f32[16,80,128]{2,1,0:T(8,128)S(1)} async-done(((f32[16,80,128]{2,1,0:T(8,128)}), f32[16,80,128]{2,1,0:T(8,128)S(1)}, u32[]{:S(2)}, u32[]{:S(2)}) %all-to-all-start.1) | async-done | bytes 655392 | tf_op jit(solution)/shard_map/all_to_all | solution.py:287
  48.1 0.0 copy-start
  48.1 12.2 %all-to-all-start = ((f32[16,64,128]{2,1,0:T(8,128)}), f32[16,64,128]{2,1,0:T(8,128)S(1)}, u32[]{:S(2)}, u32[]{:S(2)}) async-start(f32[16,64,128]{2,1,0:T(8,128)} %pack.2), calls=%async_computation | async-start | bytes 1048576 | tf_op jit(solution)/shard_map/all_to_all | solution.py:287
  60.4 0.0 copy-done
  60.4 23.0 %sums.2 = (f32[32,72,128]{2,1,0:T(8,128)}, f32[32,72,128]{2,1,0:T(8,128)}) custom-call(s32[1]{0:T(128)} %bitcast.refs_0_, f32[16,80,128]{2,1,0:T(8,128)} %copy-done), custom_call_target="tpu_custom_call" | custom-call | flops 16000000000 | bytes 32000000 | tf_op jit(solution)/shard_map/sums/pallas_call | solution.py:235
  83.3 0.0 all-to-all-done.refs_1_
  83.3 0.0 copy-start.1
  83.3 0.8 copy-done.1
  84.1 18.9 %sums.3 = (f32[32,72,128]{2,1,0:T(8,128)}, f32[32,72,128]{2,1,0:T(8,128)}) custom-call(s32[1]{0:T(128)} %bitcast.refs_0_, f32[16,64,128]{2,1,0:T(8,128)} %copy-done.1, f32[32,72,128]{2,1,0:T(8,128)} %get-tuple-element.8.refs_2_, f32[32,72,128]{2,1,0:T(8,128)} %get-tuple-element.9.refs_3_), custom_call_target="tpu_custom_call" | custom-call | flops 12000000000 | bytes 24000000 | tf_op jit(solution)/shard_map/sums/pallas_call | solution.py:235
  103.1 8.9 %collective-permute-start = (f32[32,72,128]{2,1,0:T(8,128)}, f32[32,72,128]{2,1,0:T(8,128)S(1)}, u32[]{:S(2)}, u32[]{:S(2)}) collective-permute-start(f32[32,72,128]{2,1,0:T(8,128)} %get-tuple-element.11), channel_id=1, source_target_pairs={{0,1},{1,0},{2,3},{3,2},{4,5},{5,4},{6,7},{7,6},{8,9},{9,8},{10,11... | collective-permute-start | bytes 3538952 | tf_op jit(solution)/shard_map/ppermute | solution.py:300
  112.0 2.7 %collective-permute-done = f32[32,72,128]{2,1,0:T(8,128)S(1)} collective-permute-done((f32[32,72,128]{2,1,0:T(8,128)}, f32[32,72,128]{2,1,0:T(8,128)S(1)}, u32[]{:S(2)}, u32[]{:S(2)}) %collective-permute-start) | collective-permute-done | bytes 1179680 | tf_op jit(solution)/shard_map/ppermute | solution.py:300
  114.6 1.4 add.3
  116.0 26.0 %all_to_all.25.parts_ref = f32[32,72,128]{2,1,0:T(8,128)} all-to-all(f32[32,72,128]{2,1,0:T(8,128)S(1)} %add.3), channel_id=1, replica_groups=mesh['far'=8,'near'=2,'cb'=16,'row'=2] {'near','cb'}, dimensions={0} | all-to-all | bytes 2359296 | tf_op jit(solution)/shard_map/all_to_all | solution.py:287
  142.0 2.1 %owned.1 = f32[8,72,128]{2,1,0:T(8,128)} custom-call(f32[32,72,128]{2,1,0:T(8,128)} %all_to_all.25.parts_ref), custom_call_target="tpu_custom_call" | custom-call | tf_op jit(solution)/shard_map/owned/pallas_call | solution.py:281
  144.1 22.8 %all_to_all.26.parts_ref = f32[8,72,128]{2,1,0:T(8,128)} all-to-all(f32[8,72,128]{2,1,0:T(8,128)} %owned.1), channel_id=1, replica_groups=mesh['far'=8,'near'=2,'cb'=16,'row'=2] {'far'}, dimensions={0} | all-to-all | bytes 589824 | tf_op jit(solution)/shard_map/all_to_all | solution.py:287
  166.9 1.8 finish.1
  168.8 14.2 %all_to_all.27 = f32[4,64,128]{2,1,0:T(8,128)S(1)} all-to-all(f32[4,64,128]{2,1,0:T(8,128)} %get-tuple-element.12), channel_id=1, replica_groups=mesh['far'=8,'near'=2,'cb'=16,'row'=2] {'near','row'}, dimensions={0} | all-to-all | bytes 262144 | tf_op jit(solution)/shard_map/all_to_all | solution.py:287
  182.9 0.7 copy.6
Async XLA Ops:
  3.5 44.6 %all-to-all-start.1 = ((f32[16,80,128]{2,1,0:T(8,128)}), f32[16,80,128]{2,1,0:T(8,128)S(1)}, u32[]{:S(2)}, u32[]{:S(2)}) async-start(f32[16,80,128]{2,1,0:T(8,128)} %pack.3), calls=%async_computation.1 | async-start | bytes 1310720 | tf_op jit(solution)/shard_map/all_to_all | solution.py:287
  48.1 12.2 %copy-start = (f32[16,80,128]{2,1,0:T(8,128)}, f32[16,80,128]{2,1,0:T(8,128)S(1)}, u32[]{:S(2)}) copy-start(f32[16,80,128]{2,1,0:T(8,128)S(1)} %all-to-all-done.1.refs_1_) | copy-start | bytes 1966084
  48.1 35.2 %all-to-all-start = ((f32[16,64,128]{2,1,0:T(8,128)}), f32[16,64,128]{2,1,0:T(8,128)S(1)}, u32[]{:S(2)}, u32[]{:S(2)}) async-start(f32[16,64,128]{2,1,0:T(8,128)} %pack.2), calls=%async_computation | async-start | bytes 1048576 | tf_op jit(solution)/shard_map/all_to_all | solution.py:287
  83.3 0.8 copy-start.1
  103.1 11.6 %collective-permute-start = (f32[32,72,128]{2,1,0:T(8,128)}, f32[32,72,128]{2,1,0:T(8,128)S(1)}, u32[]{:S(2)}, u32[]{:S(2)}) collective-permute-start(f32[32,72,128]{2,1,0:T(8,128)} %get-tuple-element.11), channel_id=1, source_target_pairs={{0,1},{1,0},{2,3},{3,2},{4,5},{5,4},{6,7},{7,6},{8,9},{9,8},{10,11... | collective-permute-start | bytes 3538952 | tf_op jit(solution)/shard_map/ppermute | solution.py:300

commit v4 on v3

--- a/solution.py
+++ b/solution.py
@@ -20,10 +20,12 @@
 PIECE = 128 // NEAR
 SOURCES = NEAR * FAR
 TILES = 14
-CHUNKS = (8, 6)
+CHUNKS = (9, 5)
+BINNED = (7, 7)
+LATE = CHUNKS[0] - BINNED[0]
 ACCS = 8
 ITEMS = 4
-SCRATCH = 2 + 3 * ACCS + ITEMS
+SCRATCH = 4 + 3 * ACCS + ITEMS
 CODE_ROWS = CODES // 16
 
 
@@ -39,8 +41,16 @@
     return [pl.BlockSpec(memory_space=pltpu.VMEM)] * count
 
 
-def chunk_rows(tiles):
-    return -(-10 * tiles // 8) * 8
+def chunk_rows(chunk):
+    return -(-(9 * CHUNKS[chunk] + BINNED[chunk]) // 8) * 8
+
+
+def place_in(counts, t):
+    chunk = 0
+    while t >= counts[chunk]:
+        t -= counts[chunk]
+        chunk += 1
+    return chunk, t
 
 
 def pack_kernel(wanted, weights_ref, codes_ref, bins_ref, out, lists_ref):
@@ -68,22 +78,21 @@
     for tile in range(56):
         for b in range(4):
             target, t = divmod(4 * tile + b, TILES)
-            chunk = 0
-            while t >= CHUNKS[chunk]:
-                t -= CHUNKS[chunk]
-                chunk += 1
-            if chunk != wanted:
-                continue
+            chunk, at = place_in(CHUNKS, t)
             tiles = CHUNKS[chunk]
-            out[target, 8 * t : 8 * t + 8, :] = blocks[b][8 * tile : 8 * tile + 8, :]
-            out[target, 8 * tiles + t : 8 * tiles + t + 1, :] = spread(tile, 16 * b)
-            out[target, 9 * tiles + t : 9 * tiles + t + 1, :] = spread(tile, 64 + 16 * b)
+            if chunk == wanted:
+                out[target, 8 * at : 8 * at + 8, :] = blocks[b][8 * tile : 8 * tile + 8, :]
+                out[target, 8 * tiles + at : 8 * tiles + at + 1, :] = spread(tile, 16 * b)
+            chunk, at = place_in(BINNED, t)
+            at += 9 * CHUNKS[chunk]
+            if chunk == wanted:
+                out[target, at : at + 1, :] = spread(tile, 64 + 16 * b)
 
 
 def pack(wanted, weights, codes, bins):
     return pl.pallas_call(
         functools.partial(pack_kernel, wanted),
-        out_shape=jax.ShapeDtypeStruct((SOURCES, chunk_rows(CHUNKS[wanted]), 128), F32),
+        out_shape=jax.ShapeDtypeStruct((SOURCES, chunk_rows(wanted), 128), F32),
         in_specs=vmem(3),
         out_specs=pl.BlockSpec(memory_space=pltpu.VMEM),
         cost_estimate=pl.CostEstimate(flops=10**9, bytes_accessed=2 * 10**6, transcendentals=0),
@@ -92,21 +101,26 @@
     )(weights, codes, bins)
 
 
-def sums_kernel(tiles, first, *refs):
-    side_ref, parts_ref = refs[:2]
-    inputs = 2 if first else 4
+def sums_kernel(chunk, *refs):
+    tiles, binned, first = CHUNKS[chunk], BINNED[chunk], chunk == 0
+    inputs = 2 if first else 5
+    outputs = 3 if first else 2
+    side_ref, sent_ref = refs[:2]
     keep_ref, send_ref = refs[inputs : inputs + 2]
-    scratch = refs[inputs + 2 : inputs + 2 + SCRATCH]
+    scratch = refs[inputs + outputs :]
+    at_sems, directions_ref, parts_ref, part_sem = scratch[:4]
+    rows_refs, at_refs = scratch[4 : 4 + ACCS], scratch[4 + ACCS : 4 + 2 * ACCS]
+    accs, items = scratch[4 + 2 * ACCS : 4 + 3 * ACCS], scratch[4 + 3 * ACCS : SCRATCH]
+    arrival = pltpu.make_async_copy(sent_ref, parts_ref, part_sem)
+    arrival.start()
     loads = []
-    before = refs[inputs + 2 + SCRATCH :]
+    before = scratch[SCRATCH:]
     if not first:
         sums_sems, before = before[0], before[1:]
         loads = [pltpu.make_async_copy(refs[2 + i], before[i], sums_sems.at[i]) for i in range(2)]
         for load in loads:
             load.start()
-    at_sems, directions_ref = scratch[0], scratch[1]
-    rows_refs, at_refs = scratch[2 : 2 + ACCS], scratch[2 + ACCS : 2 + 2 * ACCS]
-    accs, items = scratch[2 + 2 * ACCS : 2 + 3 * ACCS], scratch[2 + 3 * ACCS :]
+    arrival.wait()
     lane = iota((8, 128), 1)
     place = iota((8, 128), 0)
     inner = jnp.bitwise_and(lane, 7)
@@ -130,38 +144,24 @@
             for acc in accs:
                 acc[pl.ds(pl.multiple_of(8 * (start + i), 8), 8), :] = jnp.zeros((8, 128), F32)
 
-    def rotate(t, carry):
-        z = [parts_ref[h, pl.ds(pl.multiple_of(8 * t, 8), 8), :] for h in range(SOURCES)]
-        for bit in range(4):
-            d = 1 << bit
-            z = [z[h ^ d] - z[h] if h & d else z[h] + z[h ^ d] for h in range(SOURCES)]
-        rotated = jnp.concatenate(z, axis=0) * SCALING
-        squares = jnp.dot(
-            rotated * rotated, group, precision=lax.Precision.HIGHEST, preferred_element_type=F32
-        )
-        floored = jnp.maximum(jnp.sqrt(squares), 1.0)
-        directions = rotated / floored
-        logs = jnp.log(floored)
-        packed = []
+    def bins_of(row):
+        sums = []
         for half in range(2):
-            log_sum = jnp.zeros((8, 128), F32)
             bin_sum = jnp.zeros((8, 128), I32)
             for j in range(8):
-                h = 8 * half + j
-                bins = jnp.broadcast_to(parts_ref[h, pl.ds(9 * tiles + t, 1), :], (8, 128)).astype(I32)
-                bins = lanes_at(bins, 8 * outer + place)
-                log_sum = log_sum + jnp.where(inner == j, logs[8 * h : 8 * h + 8], 0.0)
+                bins = parts_ref[8 * half + j, pl.ds(9 * tiles + row, 1), :]
+                bins = lanes_at(jnp.broadcast_to(bins, (8, 128)).astype(I32), 8 * outer + place)
                 bin_sum = bin_sum + jnp.where(inner == j, bins, 0)
-            packed.append((log_sum, bin_sum))
-        for h in range(SOURCES):
-            directions_ref[SOURCES * t + h] = directions[8 * h : 8 * h + 8]
-        base = packed[0][1] >> 4
+            sums.append(bin_sum)
+        return sums
+
+    def counted(log_sums, bin_sums, carry):
+        base = bin_sums[0] >> 4
         low, high, low_count, high_count = carry
         for offset in range(16):
-            clear(t, offset)
             log_total = jnp.zeros((8, 128), F32)
             count = jnp.zeros((8, 128), F32)
-            for log_sum, bin_sum in packed:
+            for log_sum, bin_sum in zip(log_sums, bin_sums):
                 chosen = jnp.bitwise_and(bin_sum, 15) == offset
                 log_total = log_total + jnp.where(chosen, log_sum, 0.0)
                 count = count + jnp.where(chosen, 1.0, 0.0)
@@ -175,8 +175,46 @@
             high_count = high_count + jnp.where(at_high, count, 0.0)
         return low, high, low_count, high_count
 
+    def rotate(t):
+        z = [parts_ref[h, pl.ds(pl.multiple_of(8 * t, 8), 8), :] for h in range(SOURCES)]
+        for bit in range(4):
+            d = 1 << bit
+            z = [z[h ^ d] - z[h] if h & d else z[h] + z[h ^ d] for h in range(SOURCES)]
+        rotated = jnp.concatenate(z, axis=0) * SCALING
+        squares = jnp.dot(
+            rotated * rotated, group, precision=lax.Precision.HIGHEST, preferred_element_type=F32
+        )
+        floored = jnp.maximum(jnp.sqrt(squares), 1.0)
+        directions = rotated / floored
+        logs = jnp.log(floored)
+        for h in range(SOURCES):
+            directions_ref[SOURCES * t + h] = directions[8 * h : 8 * h + 8]
+        for offset in range(16):
+            clear(t, offset)
+        sums = []
+        for half in range(2):
+            log_sum = jnp.zeros((8, 128), F32)
+            for j in range(8):
+                h = 8 * half + j
+                log_sum = log_sum + jnp.where(inner == j, logs[8 * h : 8 * h + 8], 0.0)
+            sums.append(log_sum)
+        return sums
+
+    def rotate_and_count(t, carry):
+        bin_sums = bins_of(t if first else t + LATE)
+        return counted(rotate(t), bin_sums, carry)
+
     empty = jnp.zeros((8, 128), F32)
-    bin_parts = lax.fori_loop(0, tiles, rotate, (empty,) * 4)
+    bin_parts = (empty,) * 4
+    if first:
+        for t in range(binned, tiles):
+            for half, log_sum in enumerate(rotate(t)):
+                refs[inputs + 2][2 * (t - binned) + half] = log_sum
+    else:
+        for row in range(LATE):
+            late = [refs[4][2 * row + half] for half in range(2)]
+            bin_parts = counted(late, bins_of(row), bin_parts)
+    bin_parts = lax.fori_loop(0, min(tiles, binned), rotate_and_count, bin_parts)
     rows = [jnp.sum(part, axis=0, keepdims=True) for part in bin_parts]
     totals = jnp.concatenate(rows + [jnp.zeros((4, 128), F32)], axis=0)
 
@@ -225,32 +263,33 @@
     lax.fori_loop(0, owners, finish, 0)
 
 
-def direction_sums(side, parts, tiles, before):
-    shape = (NEAR * CODE_ROWS // 256, PIECE + 8, 128)
+def direction_sums(side, parts, chunk, before):
+    tiles, shape = CHUNKS[chunk], (NEAR * CODE_ROWS // 256, PIECE + 8, 128)
     arrays = () if before is None else tuple(before)
-
-    def kernel(*refs):
-        sums_kernel(tiles, before is None, *refs)
-
+    later = [pltpu.SemaphoreType.DMA((2,))] + [pltpu.VMEM(shape, F32)] * 2
+    anywhere = pl.BlockSpec(memory_space=pl.ANY)
+    logs = [jax.ShapeDtypeStruct((2 * LATE, 8, 128), F32)]
     return pl.pallas_call(
-        kernel,
-        out_shape=[jax.ShapeDtypeStruct(shape, F32)] * 2,
-        in_specs=[pl.BlockSpec(memory_space=pltpu.SMEM)]
-        + vmem(1)
-        + [pl.BlockSpec(memory_space=pl.ANY)] * len(arrays),
-        out_specs=vmem(2),
+        functools.partial(sums_kernel, chunk),
+        out_shape=[jax.ShapeDtypeStruct(shape, F32)] * 2 + (logs if before is None else []),
+        in_specs=[pl.BlockSpec(memory_space=pltpu.SMEM), anywhere]
+        + ([] if before is None else [anywhere] * 2 + vmem(1)),
+        out_specs=vmem(3 if before is None else 2),
         scratch_shapes=[
             pltpu.SemaphoreType.DMA((ACCS,)),
             pltpu.VMEM((SOURCES * tiles, 8, 128), F32),
+            pltpu.VMEM(parts.shape, F32),
+            pltpu.SemaphoreType.DMA,
         ]
         + [pltpu.VMEM((2 * tiles, 128), I32)] * ACCS
         + [pltpu.SMEM((2 * tiles, 128), I32)] * ACCS
         + [pltpu.VMEM((CODE_ROWS, 128), F32)] * ACCS
         + [pltpu.VMEM((8 * ACCS, 128), F32)] * ITEMS
-        + ([] if before is None else [pltpu.SemaphoreType.DMA((2,))] + [pltpu.VMEM(shape, F32)] * 2),
+        + ([] if before is None else later),
         cost_estimate=pl.CostEstimate(
             flops=2 * 10**9 * tiles, bytes_accessed=4 * 10**6 * tiles, transcendentals=0
         ),
+        compiler_params=pltpu.CompilerParams(vmem_limit_bytes=40 << 20),
         name="sums",
     )(side, parts, *arrays)
 
@@ -279,7 +318,12 @@
 def simple(kernel, name, shapes, *arrays):
     out_shape = [jax.ShapeDtypeStruct(shape, F32) for shape in shapes]
     return pl.pallas_call(
-        kernel, out_shape=out_shape, in_specs=vmem(len(arrays)), out_specs=vmem(len(shapes)), name=name
+        kernel,
+        out_shape=out_shape,
+        in_specs=vmem(len(arrays)),
+        out_specs=vmem(len(shapes)),
+        compiler_params=pltpu.CompilerParams(vmem_limit_bytes=16 << 20),
+        name=name,
     )(*arrays)
 
 
@@ -294,8 +338,8 @@
         for chunk in range(len(CHUNKS))
     ]
     sums = None
-    for chunk, tiles in zip(received, CHUNKS):
-        sums = direction_sums(side.reshape(1), chunk, tiles, sums)
+    for chunk, parts in enumerate(received):
+        sums = direction_sums(side.reshape(1), parts, chunk, sums)
     keep, send = sums
     joined = exchanged(keep + lax.ppermute(send, "row", [(0, 1), (1, 0)]), ("near", "cb"))
     (owned,) = simple(owned_kernel, "owned", [(FAR, PIECE + 8, 128)], joined)

time: 184 us -> 175 us (0.951)
  Pallas kernels: 51.3 us -> 44 us
  waiting for transfers between devices: 28.9 us -> 31.9 us
  starting transfers between devices: 36.9 us -> 34.7 us
    pallas_call x2, Pallas kernels: 41.9 us -> 37.8 us  [direction_sums(): pl.pallas_call(functools.partial(sums_kernel, chunk), out_shape=[jax.Shap...]
    pallas_call x2, Pallas kernels: 3.9 us -> 0.71 us  [simple(): pl.pallas_call(kernel, out_shape=out_shape, in_specs=vmem(len(arrays)), o...]
    all_to_all x2, waiting for transfers between devices: 26.3 us -> 29.4 us  [exchanged(): return lax.all_to_all(array, axis, 0, 0, tiled=True)]
where the time goes in v4:
time: 175 us; the launch traced here: 174 us
  blocking collectives  62.5 us (36%)
  Pallas kernels  44 us (25%)
  starting transfers between devices  34.7 us (20%)
  waiting for transfers between devices  31.9 us (18%)
    all_to_all x3, blocking collectives, exchanged(): return lax.all_to_all(array, axis, 0, 0, tiled=True)  62.5 us
    pallas_call x2, Pallas kernels, direction_sums(): pl.pallas_call(functools.partial(sums_kernel, chunk), out_shape=[jax.Shap...  37.8 us
    all_to_all x2, waiting for transfers between devices, exchanged(): return lax.all_to_all(array, axis, 0, 0, tiled=True)  29.4 us
    all_to_all x2, starting transfers between devices, exchanged(): return lax.all_to_all(array, axis, 0, 0, tiled=True)  27.6 us
    ppermute x1, starting transfers between devices, per_device(): lax.ppermute(send, 'row', [(0, 1), (1, 0)])  7.1 us
    pallas_call x2, Pallas kernels, pack(): pl.pallas_call(functools.partial(pack_kernel, wanted), out_shape=jax.Shap...  5.51 us
  transfers between devices with their start and end apart: 3, of which 2 were waited for; matrix products, arithmetic and copies ran while one was open for 0% of the time, Pallas kernels for 14%

profile of v4, /device:TPU:1, one launch (start us, length us, event | category | flops | bytes accessed | tf_op | source)
XLA Modules:
  0.0 174.5 jit_solution(14996844096959838726)
XLA Ops:
  0.6 2.9 %pack.3 = f32[16,88,128]{2,1,0:T(8,128)} custom-call(bf16[448,512]{1,0:T(8,128)(2,1)} %weights_ref.3, s32[64,448]{1,0:T(8,128)} %bitcast.6, s32[64,448]{1,0:T(8,128)} %bitcast.8), custom_call_target="tpu_custom_call" | custom-call | flops 1000000000 | bytes 2000000 | tf_op jit(solution)/shard_map/pack/pallas_call | solution.py:93
  3.5 15.7 %all-to-all-start.1 = ((f32[16,88,128]{2,1,0:T(8,128)}), f32[16,88,128]{2,1,0:T(8,128)S(1)}, u32[]{:S(2)}, u32[]{:S(2)}) async-start(f32[16,88,128]{2,1,0:T(8,128)} %pack.3), calls=%async_computation.1 | async-start | bytes 1441792 | tf_op jit(solution)/shard_map/all_to_all | solution.py:331
  19.3 2.6 %pack.2 = f32[16,56,128]{2,1,0:T(8,128)} custom-call(bf16[448,512]{1,0:T(8,128)(2,1)} %weights_ref.3, s32[64,448]{1,0:T(8,128)} %bitcast.7, s32[64,448]{1,0:T(8,128)} %bitcast.9), custom_call_target="tpu_custom_call" | custom-call | flops 1000000000 | bytes 2000000 | tf_op jit(solution)/shard_map/pack/pallas_call | solution.py:93
  21.9 29.4 %all-to-all-done.1.refs_1_ = f32[16,88,128]{2,1,0:T(8,128)S(1)} async-done(((f32[16,88,128]{2,1,0:T(8,128)}), f32[16,88,128]{2,1,0:T(8,128)S(1)}, u32[]{:S(2)}, u32[]{:S(2)}) %all-to-all-start.1) | async-done | bytes 720928 | tf_op jit(solution)/shard_map/all_to_all | solution.py:331
  51.3 11.9 %all-to-all-start = ((f32[16,56,128]{2,1,0:T(8,128)}), f32[16,56,128]{2,1,0:T(8,128)S(1)}, u32[]{:S(2)}, u32[]{:S(2)}) async-start(f32[16,56,128]{2,1,0:T(8,128)} %pack.2), calls=%async_computation | async-start | bytes 917504 | tf_op jit(solution)/shard_map/all_to_all | solution.py:331
  63.2 22.5 %sums.2 = (f32[32,72,128]{2,1,0:T(8,128)S(1)}, f32[32,72,128]{2,1,0:T(8,128)S(1)}, f32[4,8,128]{2,1,0:T(8,128)S(1)}) custom-call(s32[1]{0:T(128)} %bitcast.refs_0_, f32[16,88,128]{2,1,0:T(8,128)S(1)} %all-to-all-done.1.refs_1_), custom_call_target="tpu_custom_call" | custom-call | flops 17999998976 | bytes 36000000 | tf_op jit(solution)/shard_map/sums/pallas_call | solution.py:272
  85.7 0.0 all-to-all-done.refs_1_
  85.7 15.2 %sums.3 = (f32[32,72,128]{2,1,0:T(8,128)S(1)}, f32[32,72,128]{2,1,0:T(8,128)S(1)}) custom-call(s32[1]{0:T(128)} %bitcast.refs_0_, f32[16,56,128]{2,1,0:T(8,128)S(1)} %all-to-all-done.refs_1_, f32[32,72,128]{2,1,0:T(8,128)S(1)} %get-tuple-element.9.refs_2_, f32[32,72,128]{2,1,0:T(8,128)S(1)} %get-tuple-element.10.refs_3_, ...), custom_call_target="tpu_custom_call" | custom-call | flops 10000000000 | bytes 20000000 | tf_op jit(solution)/shard_map/sums/pallas_call | solution.py:272
  101.0 7.1 %collective-permute-start = (f32[32,72,128]{2,1,0:T(8,128)S(1)}, f32[32,72,128]{2,1,0:T(8,128)S(1)}, u32[]{:S(2)}, u32[]{:S(2)}) collective-permute-start(f32[32,72,128]{2,1,0:T(8,128)S(1)} %get-tuple-element.13), channel_id=1, source_target_pairs={{0,1},{1,0},{2,3},{3,2},{4,5},{5,4},{6,7},{7,6},{8,9},{9,8},{10,11... | collective-permute-start | bytes 3538952 | tf_op jit(solution)/shard_map/ppermute | solution.py:344
  108.1 2.5 %collective-permute-done = f32[32,72,128]{2,1,0:T(8,128)S(1)} collective-permute-done((f32[32,72,128]{2,1,0:T(8,128)S(1)}, f32[32,72,128]{2,1,0:T(8,128)S(1)}, u32[]{:S(2)}, u32[]{:S(2)}) %collective-permute-start) | collective-permute-done | bytes 1179680 | tf_op jit(solution)/shard_map/ppermute | solution.py:344
  110.6 0.1 add.3
  110.7 25.0 %all_to_all.25.parts_ref = f32[32,72,128]{2,1,0:T(8,128)S(1)} all-to-all(f32[32,72,128]{2,1,0:T(8,128)S(1)} %add.3), channel_id=1, replica_groups=mesh['far'=8,'near'=2,'cb'=16,'row'=2] {'near','cb'}, dimensions={0} | all-to-all | bytes 2359296 | tf_op jit(solution)/shard_map/all_to_all | solution.py:331
  135.7 0.1 owned.1
  135.7 24.2 %all_to_all.26.parts_ref = f32[8,72,128]{2,1,0:T(8,128)S(1)} all-to-all(f32[8,72,128]{2,1,0:T(8,128)S(1)} %owned.1), channel_id=1, replica_groups=mesh['far'=8,'near'=2,'cb'=16,'row'=2] {'far'}, dimensions={0} | all-to-all | bytes 589824 | tf_op jit(solution)/shard_map/all_to_all | solution.py:331
  160.0 0.6 finish.1
  160.6 13.2 %all_to_all.27 = f32[4,64,128]{2,1,0:T(8,128)S(1)} all-to-all(f32[4,64,128]{2,1,0:T(8,128)S(1)} %get-tuple-element.14), channel_id=1, replica_groups=mesh['far'=8,'near'=2,'cb'=16,'row'=2] {'near','row'}, dimensions={0} | all-to-all | bytes 262144 | tf_op jit(solution)/shard_map/all_to_all | solution.py:331
  173.8 0.7 copy.6
Async XLA Ops:
  3.5 47.8 %all-to-all-start.1 = ((f32[16,88,128]{2,1,0:T(8,128)}), f32[16,88,128]{2,1,0:T(8,128)S(1)}, u32[]{:S(2)}, u32[]{:S(2)}) async-start(f32[16,88,128]{2,1,0:T(8,128)} %pack.3), calls=%async_computation.1 | async-start | bytes 1441792 | tf_op jit(solution)/shard_map/all_to_all | solution.py:331
  51.3 34.4 %all-to-all-start = ((f32[16,56,128]{2,1,0:T(8,128)}), f32[16,56,128]{2,1,0:T(8,128)S(1)}, u32[]{:S(2)}, u32[]{:S(2)}) async-start(f32[16,56,128]{2,1,0:T(8,128)} %pack.2), calls=%async_computation | async-start | bytes 917504 | tf_op jit(solution)/shard_map/all_to_all | solution.py:331
  101.0 9.6 %collective-permute-start = (f32[32,72,128]{2,1,0:T(8,128)S(1)}, f32[32,72,128]{2,1,0:T(8,128)S(1)}, u32[]{:S(2)}, u32[]{:S(2)}) collective-permute-start(f32[32,72,128]{2,1,0:T(8,128)S(1)} %get-tuple-element.13), channel_id=1, source_target_pairs={{0,1},{1,0},{2,3},{3,2},{4,5},{5,4},{6,7},{7,6},{8,9},{9,8},{10,11... | collective-permute-start | bytes 3538952 | tf_op jit(solution)/shard_map/ppermute | solution.py:344

commit v5 on v4

--- a/solution.py
+++ b/solution.py
@@ -20,8 +20,8 @@
 PIECE = 128 // NEAR
 SOURCES = NEAR * FAR
 TILES = 14
-CHUNKS = (9, 5)
-BINNED = (7, 7)
+CHUNKS = (10, 4)
+BINNED = (6, 8)
 LATE = CHUNKS[0] - BINNED[0]
 ACCS = 8
 ITEMS = 4

time: 175 us -> 179 us (1.023)
  blocking collectives: 62.5 us -> 67 us
  starting transfers between devices: 34.7 us -> 30.4 us
  waiting for transfers between devices: 31.9 us -> 34.5 us
    all_to_all x3, blocking collectives: 62.5 us -> 67 us  [exchanged(): return lax.all_to_all(array, axis, 0, 0, tiled=True)]
    ppermute x1, starting transfers between devices: 7.1 us -> 2.57 us  [per_device(): lax.ppermute(send, 'row', [(0, 1), (1, 0)])]
    all_to_all x2, waiting for transfers between devices: 29.4 us -> 32 us  [exchanged(): return lax.all_to_all(array, axis, 0, 0, tiled=True)]
  transfers between devices with their start and end apart: 3 -> 3, of which waited for: 2 -> 2; matrix products, arithmetic and copies ran while one was open for 0% -> 0% of each run, Pallas kernels for 14% -> 15%
where the time goes in v5:
time: 179 us; the launch traced here: 178 us
  blocking collectives  67 us (37%)
  Pallas kernels  43.6 us (24%)
  waiting for transfers between devices  34.5 us (19%)
  starting transfers between devices  30.4 us (17%)
  local copies, waits for them, and re-layouts  2.02 us (1%)
    all_to_all x3, blocking collectives, exchanged(): return lax.all_to_all(array, axis, 0, 0, tiled=True)  67 us
    pallas_call x2, Pallas kernels, direction_sums(): pl.pallas_call(functools.partial(sums_kernel, chunk), out_shape=[jax.Shap...  37.4 us
    all_to_all x2, waiting for transfers between devices, exchanged(): return lax.all_to_all(array, axis, 0, 0, tiled=True)  32 us
    all_to_all x2, starting transfers between devices, exchanged(): return lax.all_to_all(array, axis, 0, 0, tiled=True)  27.8 us
    pallas_call x2, Pallas kernels, pack(): pl.pallas_call(functools.partial(pack_kernel, wanted), out_shape=jax.Shap...  5.51 us
  transfers between devices with their start and end apart: 3, of which 2 were waited for; matrix products, arithmetic and copies ran while one was open for 0% of the time, Pallas kernels for 15%

profile of v5, /device:TPU:1, one launch (start us, length us, event | category | flops | bytes accessed | tf_op | source)
XLA Modules:
  0.0 178.4 jit_solution(16064881365183157293)
XLA Ops:
  0.6 2.9 %pack.3 = f32[16,96,128]{2,1,0:T(8,128)} custom-call(bf16[448,512]{1,0:T(8,128)(2,1)} %weights_ref.3, s32[64,448]{1,0:T(8,128)} %bitcast.6, s32[64,448]{1,0:T(8,128)} %bitcast.8), custom_call_target="tpu_custom_call" | custom-call | flops 1000000000 | bytes 2000000 | tf_op jit(solution)/shard_map/pack/pallas_call | solution.py:93
  3.5 15.7 %all-to-all-start.1 = ((f32[16,96,128]{2,1,0:T(8,128)}), f32[16,96,128]{2,1,0:T(8,128)S(1)}, u32[]{:S(2)}, u32[]{:S(2)}) async-start(f32[16,96,128]{2,1,0:T(8,128)} %pack.3), calls=%async_computation.1 | async-start | bytes 1572864 | tf_op jit(solution)/shard_map/all_to_all | solution.py:331
  19.3 2.6 %pack.2 = f32[16,48,128]{2,1,0:T(8,128)} custom-call(bf16[448,512]{1,0:T(8,128)(2,1)} %weights_ref.3, s32[64,448]{1,0:T(8,128)} %bitcast.7, s32[64,448]{1,0:T(8,128)} %bitcast.9), custom_call_target="tpu_custom_call" | custom-call | flops 1000000000 | bytes 2000000 | tf_op jit(solution)/shard_map/pack/pallas_call | solution.py:93
  21.9 32.0 %all-to-all-done.1.refs_1_ = f32[16,96,128]{2,1,0:T(8,128)S(1)} async-done(((f32[16,96,128]{2,1,0:T(8,128)}), f32[16,96,128]{2,1,0:T(8,128)S(1)}, u32[]{:S(2)}, u32[]{:S(2)}) %all-to-all-start.1) | async-done | bytes 786464 | tf_op jit(solution)/shard_map/all_to_all | solution.py:331
  53.9 12.1 %all-to-all-start = ((f32[16,48,128]{2,1,0:T(8,128)}), f32[16,48,128]{2,1,0:T(8,128)S(1)}, u32[]{:S(2)}, u32[]{:S(2)}) async-start(f32[16,48,128]{2,1,0:T(8,128)} %pack.2), calls=%async_computation | async-start | bytes 786432 | tf_op jit(solution)/shard_map/all_to_all | solution.py:331
  66.0 24.2 %sums.2 = (f32[32,72,128]{2,1,0:T(8,128)S(1)}, f32[32,72,128]{2,1,0:T(8,128)S(1)}, f32[8,8,128]{2,1,0:T(8,128)S(1)}) custom-call(s32[1]{0:T(128)} %bitcast.refs_0_, f32[16,96,128]{2,1,0:T(8,128)S(1)} %all-to-all-done.1.refs_1_), custom_call_target="tpu_custom_call" | custom-call | flops 20000000000 | bytes 40000000 | tf_op jit(solution)/shard_map/sums/pallas_call | solution.py:272
  90.2 0.0 copy-start
  90.2 0.6 copy-done
  90.8 0.0 all-to-all-done.refs_1_
  90.8 0.0 copy-start.1
  90.8 0.8 copy-done.1
  91.6 13.2 %sums.3 = (f32[32,72,128]{2,1,0:T(8,128)S(1)}, f32[32,72,128]{2,1,0:T(8,128)S(1)}) custom-call(s32[1]{0:T(128)} %bitcast.refs_0_, f32[16,48,128]{2,1,0:T(8,128)S(1)} %all-to-all-done.refs_1_, f32[32,72,128]{2,1,0:T(8,128)S(1)} %get-tuple-element.9.refs_2_, f32[32,72,128]{2,1,0:T(8,128)S(1)} %get-tuple-element.10.refs_3_, f32[8,8,128]{2,1,0:T(8,128)S(1)} %copy-done.1), custom_call_target="tpu_custom_call" | custom-call | flops 8000000000 | bytes 16000000 | tf_op jit(solution)/shard_map/sums/pallas_call | solution.py:272
  104.8 2.6 %collective-permute-start = (f32[32,72,128]{2,1,0:T(8,128)S(1)}, f32[32,72,128]{2,1,0:T(8,128)S(1)}, u32[]{:S(2)}, u32[]{:S(2)}) collective-permute-start(f32[32,72,128]{2,1,0:T(8,128)S(1)} %get-tuple-element.13), channel_id=1, source_target_pairs={{0,1},{1,0},{2,3},{3,2},{4,5},{5,4},{6,7},{7,6},{8,9},{9,8},{10,11... | collective-permute-start | bytes 3538952 | tf_op jit(solution)/shard_map/ppermute | solution.py:344
  107.4 2.5 %collective-permute-done = f32[32,72,128]{2,1,0:T(8,128)S(1)} collective-permute-done((f32[32,72,128]{2,1,0:T(8,128)S(1)}, f32[32,72,128]{2,1,0:T(8,128)S(1)}, u32[]{:S(2)}, u32[]{:S(2)}) %collective-permute-start) | collective-permute-done | bytes 1179680 | tf_op jit(solution)/shard_map/ppermute | solution.py:344
  109.9 0.1 add.3
  110.0 26.3 %all_to_all.25.parts_ref = f32[32,72,128]{2,1,0:T(8,128)S(1)} all-to-all(f32[32,72,128]{2,1,0:T(8,128)S(1)} %add.3), channel_id=1, replica_groups=mesh['far'=8,'near'=2,'cb'=16,'row'=2] {'near','cb'}, dimensions={0} | all-to-all | bytes 2359296 | tf_op jit(solution)/shard_map/all_to_all | solution.py:331
  136.3 0.1 owned.1
  136.4 27.4 %all_to_all.26.parts_ref = f32[8,72,128]{2,1,0:T(8,128)S(1)} all-to-all(f32[8,72,128]{2,1,0:T(8,128)S(1)} %owned.1), channel_id=1, replica_groups=mesh['far'=8,'near'=2,'cb'=16,'row'=2] {'far'}, dimensions={0} | all-to-all | bytes 589824 | tf_op jit(solution)/shard_map/all_to_all | solution.py:331
  163.8 0.6 finish.1
  164.5 13.2 %all_to_all.27 = f32[4,64,128]{2,1,0:T(8,128)S(1)} all-to-all(f32[4,64,128]{2,1,0:T(8,128)S(1)} %get-tuple-element.14), channel_id=1, replica_groups=mesh['far'=8,'near'=2,'cb'=16,'row'=2] {'near','row'}, dimensions={0} | all-to-all | bytes 262144 | tf_op jit(solution)/shard_map/all_to_all | solution.py:331
  177.7 0.7 copy.6
Async XLA Ops:
  3.5 50.4 %all-to-all-start.1 = ((f32[16,96,128]{2,1,0:T(8,128)}), f32[16,96,128]{2,1,0:T(8,128)S(1)}, u32[]{:S(2)}, u32[]{:S(2)}) async-start(f32[16,96,128]{2,1,0:T(8,128)} %pack.3), calls=%async_computation.1 | async-start | bytes 1572864 | tf_op jit(solution)/shard_map/all_to_all | solution.py:331
  53.9 36.9 %all-to-all-start = ((f32[16,48,128]{2,1,0:T(8,128)}), f32[16,48,128]{2,1,0:T(8,128)S(1)}, u32[]{:S(2)}, u32[]{:S(2)}) async-start(f32[16,48,128]{2,1,0:T(8,128)} %pack.2), calls=%async_computation | async-start | bytes 786432 | tf_op jit(solution)/shard_map/all_to_all | solution.py:331
  90.2 0.6 copy-start
  90.8 0.8 copy-start.1
  104.8 5.0 %collective-permute-start = (f32[32,72,128]{2,1,0:T(8,128)S(1)}, f32[32,72,128]{2,1,0:T(8,128)S(1)}, u32[]{:S(2)}, u32[]{:S(2)}) collective-permute-start(f32[32,72,128]{2,1,0:T(8,128)S(1)} %get-tuple-element.13), channel_id=1, source_target_pairs={{0,1},{1,0},{2,3},{3,2},{4,5},{5,4},{6,7},{7,6},{8,9},{9,8},{10,11... | collective-permute-start | bytes 3538952 | tf_op jit(solution)/shard_map/ppermute | solution.py:344
